TPU v7x, 768 devices: a whole 4x8x12 slice. The times are simulated.
768 devices in a mesh: dp: 192 (over x, y, z_lo, core), seq: 4 (over z_hi).
Axes of the slice: x: 4, y: 8, z: 12 (z_hi: 4, z_lo: 3; z = z_hi * 3 + z_lo), core: 2. Of those that a mesh axis runs over, the one named last changes fastest.
Arguments:
- image_query: bfloat16 [192, 256, 1536], P('dp', 'seq'), may hold values from -300 to 300
- image_key: bfloat16 [192, 256, 1536], P('dp', 'seq'), may hold values from -300 to 300
- image_value: bfloat16 [192, 256, 1536], P('dp', 'seq'), may hold values from -6 to 6
- text_key: bfloat16 [192, 512, 1536], P('dp', 'seq'), may hold values from -300 to 300
- text_value: bfloat16 [192, 512, 1536], P('dp', 'seq'), may hold values from -6 to 6
- query_gain: float32 [128], replicated, may hold values from 0.6 to 1.8
- key_gain: float32 [128], replicated, may hold values from 0.6 to 1.8
- embed_weight: bfloat16 [1536, 1408], replicated, may hold values from -0.15625 to 0.15625
- position_embed: float32 [64, 1408], replicated, may hold values from -2.7 to 2.7
- norm_gain: float32 [1408], replicated, may hold values from 0.25 to 1.75
- final_gain: float32 [1408], replicated, may hold values from 0.25 to 1.75
- up_weight: bfloat16 [3072, 1408], P(('dp', 'seq')), may hold values from -0.15625 to 0.15625
- down_weight: bfloat16 [3072, 1408], P(('dp', 'seq')), may hold values from -0.109375 to 0.109375
- reward_direction: float32 [1408], replicated, may hold values from -1.5 to 1.5
Outputs:
- attended: bfloat16 [192, 256, 1536], P('dp', None, 'seq')
- attended_gradient: bfloat16 [192, 256, 1536], P('dp', None, 'seq')
- reward: float32 [192], P('dp')
All inputs are finite; a program needn't handle non-finite values.
Results may differ from a plain program's by a relative error of at most 0.02.
Values may be sent and summed in bfloat16 or wider, within the bound.
No kernel may reach another device: no remote copies, remote signals or barrier semaphores. Data moves between devices by JAX's collectives and lax.ppermute only.
A program may use at most 64 MiB of HBM per device.

v0:
```python
import math

import jax
import jax.numpy as jnp
from jax import lax
from jax.sharding import PartitionSpec as P

HEAD = 128
PATCH_W = 32


epsilon = 1e-06
root_half = 0.7071067811865476
inv_root_tau = 0.3989422804014327


def norm_heads(features, gain_vector):
    token_count = features.shape[0]
    grouped = features.astype(jnp.float32).reshape(token_count, -1, HEAD)
    inverse_rms = lax.rsqrt(jnp.mean(grouped * grouped, axis=-1, keepdims=True) + epsilon)
    return (grouped * inverse_rms * gain_vector).astype(jnp.bfloat16)


def layer_stats(residual):
    centered = residual - jnp.mean(residual, axis=-1, keepdims=True)
    inverse_std = lax.rsqrt(jnp.mean(centered * centered, axis=-1, keepdims=True) + epsilon)
    return (centered * inverse_std, inverse_std)


def layer_back(upstream, normed, inverse_std):
    return inverse_std * (
        upstream
        - jnp.mean(upstream, axis=-1, keepdims=True)
        - normed * jnp.mean(upstream * normed, axis=-1, keepdims=True)
    )


def gelu_parts(preact):
    cumulative = 0.5 * (1.0 + lax.erf(preact * root_half))
    activation = preact * cumulative
    derivative = cumulative + preact * jnp.exp(-0.5 * preact * preact) * inv_root_tau
    return (activation, derivative)


def pool_patches(attended):
    token_count, feature_width = attended.shape
    patch_grid = attended.astype(jnp.float32).reshape(
        token_count // PATCH_W // 2, 2, PATCH_W // 2, 2, feature_width
    )
    return jnp.mean(patch_grid, axis=(1, 3)).reshape(-1, feature_width).astype(jnp.bfloat16)


def spread_patches(pooled_slope):
    pooled_count, feature_width = pooled_slope.shape
    row_count = pooled_count // (PATCH_W // 2)
    patch_grid = pooled_slope.reshape(row_count, 1, PATCH_W // 2, 1, feature_width)
    patch_grid = jnp.broadcast_to(0.25 * patch_grid, (row_count, 2, PATCH_W // 2, 2, feature_width))
    return patch_grid.reshape(4 * pooled_count, feature_width).astype(jnp.bfloat16)


def contract_rows(left_side, right_side):
    return lax.dot_general(
        left_side, right_side, (((1,), (1,)), ((), ())), preferred_element_type=jnp.float32
    )


def round_term(partial_sum):
    return lax.optimization_barrier(partial_sum.astype(jnp.bfloat16)).astype(jnp.float32)


def attend(queries, key_heads, value_heads):
    query_count = queries.shape[0]
    block_rows = math.gcd(query_count, 512)
    query_blocks = queries.reshape(query_count // block_rows, block_rows, queries.shape[1], HEAD)

    def one_block(query_block):
        scores = jnp.einsum(
            "qhd,khd->hqk", query_block, key_heads, preferred_element_type=jnp.float32
        ) * HEAD ** (-0.5)
        exponent = jnp.exp(scores)
        attention_weights = (exponent / jnp.sum(exponent, axis=-1, keepdims=True)).astype(
            jnp.bfloat16
        )
        mixed_heads = jnp.einsum(
            "hqk,khd->qhd", attention_weights, value_heads, preferred_element_type=jnp.float32
        )
        return mixed_heads.astype(jnp.bfloat16)

    mixed_blocks = lax.map(one_block, query_blocks)
    return mixed_blocks.reshape(query_count, -1)


def on_device(
    image_query,
    image_key,
    image_value,
    text_key,
    text_value,
    query_gain,
    key_gain,
    embed_weight,
    position_embed,
    norm_gain,
    final_gain,
    up_weight,
    down_weight,
    reward_direction,
):
    exchanged = (
        lax.all_to_all(image_query, "seq", split_axis=2, concat_axis=1, tiled=True),
        lax.all_to_all(image_key, "seq", split_axis=2, concat_axis=1, tiled=True),
        lax.all_to_all(image_value, "seq", split_axis=2, concat_axis=1, tiled=True),
        lax.all_to_all(text_key, "seq", split_axis=2, concat_axis=1, tiled=True),
        lax.all_to_all(text_value, "seq", split_axis=2, concat_axis=1, tiled=True),
    )
    queries = norm_heads(exchanged[0][0], query_gain)
    key_heads = norm_heads(jnp.concatenate([exchanged[3][0], exchanged[1][0]], axis=0), key_gain)
    value_rows = jnp.concatenate([exchanged[4][0], exchanged[2][0]], axis=0)
    value_heads = value_rows.reshape(value_rows.shape[0], -1, HEAD)
    attended = attend(queries, key_heads, value_heads)
    pooled = pool_patches(attended)
    group_width = pooled.shape[1]
    embed_rows = lax.dynamic_slice_in_dim(
        embed_weight, lax.axis_index("seq") * group_width, group_width, 0
    )
    partial_embed = jnp.dot(pooled, embed_rows, preferred_element_type=jnp.float32)
    residual_in = (
        lax.psum(partial_embed.astype(jnp.bfloat16), "seq").astype(jnp.float32) + position_embed
    )
    normed_in, inverse_in = layer_stats(residual_in)
    hidden_in = (normed_in * norm_gain).astype(jnp.bfloat16)
    gathered_up, gathered_down = (
        lax.all_gather(up_weight, "dp", axis=0, tiled=True),
        lax.all_gather(down_weight, "dp", axis=0, tiled=True),
    )
    activation, derivative = gelu_parts(contract_rows(hidden_in, gathered_up))
    branch = jnp.dot(
        activation.astype(jnp.bfloat16), gathered_down, preferred_element_type=jnp.float32
    )
    residual_out = residual_in + lax.psum(round_term(branch).astype(jnp.bfloat16), "seq").astype(
        jnp.float32
    )
    normed_out, inverse_out = layer_stats(residual_out)
    direction = final_gain * reward_direction
    reward = jnp.mean(jnp.sum(normed_out * direction, axis=-1))
    out_slope = layer_back(direction, normed_out, inverse_out)
    slope_low = out_slope.astype(jnp.bfloat16)
    hidden_slope = (contract_rows(slope_low, gathered_down) * derivative).astype(jnp.bfloat16)
    slope_part = jnp.dot(hidden_slope, gathered_up, preferred_element_type=jnp.float32)
    slope_in = lax.psum(round_term(slope_part).astype(jnp.bfloat16), "seq").astype(jnp.float32)
    input_slope = out_slope + layer_back(slope_in * norm_gain, normed_in, inverse_in)
    pooled_slope = contract_rows(input_slope.astype(jnp.bfloat16), embed_rows)
    return (attended[None], spread_patches(pooled_slope)[None], reward.reshape(1))


def solution(mesh):
    return jax.shard_map(
        on_device,
        mesh=mesh,
        in_specs=(
            P("dp", "seq", None),
            P("dp", "seq", None),
            P("dp", "seq", None),
            P("dp", "seq", None),
            P("dp", "seq", None),
            P(),
            P(),
            P(),
            P(),
            P(),
            P(),
            P(("dp", "seq"), None),
            P(("dp", "seq"), None),
            P(),
        ),
        out_specs=(P("dp", None, "seq"), P("dp", None, "seq"), P("dp")),
        check_vma=False,
    )
```

profile of v0, /device:TPU:6, one launch (start us, length us, event | category | flops | bytes accessed | tf_op | source)
XLA Modules:
  0.0 2263.0 jit_solution(773888786286892817)
XLA Ops:
  8.0 2.1 copy.96
  10.6 8.8 reduce.1
  19.4 1.0 reshape.139
  20.4 14.5 all-to-all-start.4
  34.9 0.6 copy.90
  35.5 8.8 reduce.3
  44.3 1.0 reshape.143
  45.3 3.3 all-to-all-done.4
  48.6 6.3 all-to-all-start.2
  54.9 0.6 copy.86
  55.5 8.8 reduce.4
  64.3 1.0 reshape.145
  65.3 2.7 all-to-all-done.2
  68.0 7.0 all-to-all-start.1
  75.1 0.6 copy.94
  75.6 8.8 reduce.2
  84.4 0.8 reshape.141
  85.3 2.2 all-to-all-done.1
  87.5 7.4 all-to-all-start.3
  94.9 0.6 copy.84
  95.5 8.8 reduce.5
  104.3 0.8 reshape.147
  105.5 7.6 all-to-all-done.3
  113.1 3.5 all-to-all-start
  116.6 0.9 bitcast_convert_fusion.1
  122.8 12.6 all-to-all-done
  136.3 0.7 fusion
  137.0 0.7 bitcast_convert_fusion
  138.7 2.2 convolution_convert_fusion.2
  142.4 0.6 fusion.58
  143.7 60.2 %all-reduce.4.cloned.1.call-done = bf16[64,1408]{1,0:T(8,128)(2,1)} async-done(((bf16[64,1408]{1,0:T(8,128)(2,1)}), bf16[64,1408]{1,0:T(8,128)(2,1)}) %all-reduce.4.cloned.1.call-update) | async-done | bytes 180240 | tf_op jit(solution)/shard_map/psum | solution.py:128
  203.8 1.1 fusion.59
  205.1 713.3 %all-gather.5.cloned.1.call-done = bf16[192,4,1408]{2,1,0:T(4,128)(2,1)} async-done(((bf16[1,4,1408]{2,1,0:T(4,128)(2,1)}), bf16[192,4,1408]{2,1,0:T(4,128)(2,1)}) %all-gather.5.cloned.1.call-update) | async-done | bytes 2162704 | tf_op jit(solution)/shard_map/all_gather | solution.py:133
  918.4 2.6 reshape.134
  921.0 0.8 fusion.27
  921.8 979.9 %all-gather.7.cloned.1.call-done = bf16[192,4,1408]{2,1,0:T(4,128)(2,1)} async-done(((bf16[1,4,1408]{2,1,0:T(4,128)(2,1)}), bf16[192,4,1408]{2,1,0:T(4,128)(2,1)}) %all-gather.7.cloned.1.call-update) | async-done | bytes 2162704 | tf_op jit(solution)/shard_map/all_gather | solution.py:134
  1901.7 4.0 reshape.136
  1905.6 2.8 convolution_convert_fusion.1
  1908.5 269.6 %all-reduce.6.cloned.1.call-done = bf16[64,1408]{1,0:T(8,128)(2,1)} async-done(((bf16[64,1408]{1,0:T(8,128)(2,1)}), bf16[64,1408]{1,0:T(8,128)(2,1)}) %all-reduce.6.cloned.1.call-update) | async-done | bytes 180240 | tf_op jit(solution)/shard_map/psum | solution.py:140
  2178.1 1.1 fusion.57
  2179.1 1.1 multiply_reduce_fusion.2
  2180.3 1.7 multiply_reduce_fusion.4
  2182.0 3.9 convolution_convert_fusion
  2185.9 0.8 copy.103
  2187.4 63.5 %all-reduce.8.cloned.1.call-done = bf16[64,1408]{1,0:T(8,128)(2,1)} async-done(((bf16[64,1408]{1,0:T(8,128)(2,1)}), bf16[64,1408]{1,0:T(8,128)(2,1)}) %all-reduce.8.cloned.1.call-update) | async-done | bytes 180240 | tf_op jit(solution)/shard_map/psum | solution.py:150
  2250.9 1.2 fusion.17
  2252.1 1.8 fusion.7
  2254.0 0.8 convert_element_type.132
  (72 shorter events, 9.8 us)
Async XLA Ops:
  8.0 26.9 %copy-start.4 = (bf16[1,64,1536]{2,1,0:T(8,128)(2,1)S(1)}, bf16[1,64,1536]{2,1,0:T(8,128)(2,1)}, u32[]{:S(2)}) copy-start(bf16[1,64,1536]{2,1,0:T(8,128)(2,1)} %param.14) | copy-start | bytes 589828
  19.4 35.5 %copy-start.5 = (bf16[1,64,1536]{2,1,0:T(8,128)(2,1)S(1)}, bf16[1,64,1536]{2,1,0:T(8,128)(2,1)}, u32[]{:S(2)}) copy-start(bf16[1,64,1536]{2,1,0:T(8,128)(2,1)} %param.16) | copy-start | bytes 589828
  20.4 28.2 %all-to-all-start.4 = ((bf16[4,2,12288]{2,1,0:T(2,128)(2,1)}), bf16[4,2,12288]{2,1,0:T(2,128)(2,1)S(1)}, u32[]{:S(2)}, u32[]{:S(2)}) async-start(bf16[4,2,12288]{2,1,0:T(2,128)(2,1)} %reshape.139), calls=%async_computation.4 | async-start | bytes 393216 | tf_op jit(solution)/shard_map/all_to_all | solution.py:111
  44.3 30.7 %copy-start.1 = (bf16[1,128,1536]{2,1,0:T(8,128)(2,1)S(1)}, bf16[1,128,1536]{2,1,0:T(8,128)(2,1)}, u32[]{:S(2)}) copy-start(bf16[1,128,1536]{2,1,0:T(8,128)(2,1)} %param.17) | copy-start | bytes 1179652
  48.6 19.4 all-to-all-start.2
  65.3 29.6 %copy-start.2 = (bf16[1,128,1536]{2,1,0:T(8,128)(2,1)S(1)}, bf16[1,128,1536]{2,1,0:T(8,128)(2,1)}, u32[]{:S(2)}) copy-start(bf16[1,128,1536]{2,1,0:T(8,128)(2,1)} %param.18) | copy-start | bytes 1179652
  68.0 19.5 all-to-all-start.1
  87.5 25.6 %all-to-all-start.3 = ((bf16[4,2,24576]{2,1,0:T(2,128)(2,1)}), bf16[4,2,24576]{2,1,0:T(2,128)(2,1)S(1)}, u32[]{:S(2)}, u32[]{:S(2)}) async-start(bf16[4,2,24576]{2,1,0:T(2,128)(2,1)} %reshape.141), calls=%async_computation.3 | async-start | bytes 786432 | tf_op jit(solution)/shard_map/all_to_all | solution.py:113
  113.1 22.3 all-to-all-start
  116.5 87.3 %all-reduce.4.cloned.1.call-start = ((), (), s32[]{:S(2)}) async-start(), calls=%async_computation.5 | async-start | bytes 360448 | tf_op jit(solution)/shard_map/psum | solution.py:128
  119.4 1.9 copy-start.9
  122.7 13.7 copy-start.10
  137.8 4.6 copy-start.7
  137.8 4.6 copy-start.8
  137.8 66.0 %copy-start.3 = (f32[64,1408]{1,0:T(8,128)S(1)}, f32[64,1408]{1,0:T(8,128)}, u32[]{:S(2)}) copy-start(f32[64,1408]{1,0:T(8,128)} %param.22) | copy-start | bytes 1081348
  140.9 777.5 %all-gather.5.cloned.1.call-start = ((), (), s32[]{:S(2)}) async-start(), calls=%async_computation.8 | async-start | bytes 2173952 | tf_op jit(solution)/shard_map/all_gather | solution.py:133
  141.5 1760.2 %all-gather.7.cloned.1.call-start = ((), (), s32[]{:S(2)}) async-start(), calls=%async_computation.9 | async-start | bytes 2173952 | tf_op jit(solution)/shard_map/all_gather | solution.py:134
  142.1 2036.0 %all-reduce.6.cloned.1.call-start = ((), (), s32[]{:S(2)}) async-start(), calls=%async_computation.6 | async-start | bytes 360448 | tf_op jit(solution)/shard_map/psum | solution.py:140
  205.1 715.9 %copy-start.6 = (f32[1408]{0:T(1024)S(1)}, f32[1408]{0:T(1024)}, u32[]{:S(2)}) copy-start(f32[1408]{0:T(1024)} %param.23) | copy-start | bytes 16900
  1908.4 342.5 %all-reduce.8.cloned.1.call-start = ((), (), s32[]{:S(2)}) async-start(), calls=%async_computation.7 | async-start | bytes 360448 | tf_op jit(solution)/shard_map/psum | solution.py:150
  2182.0 70.1 %copy-start = (bf16[64,1408]{1,0:T(8,128)(2,1)S(1)}, bf16[64,1408]{1,0:T(8,128)(2,1)}, u32[]{:S(2)}) copy-start(bf16[64,1408]{1,0:T(8,128)(2,1)} %all-reduce.6.cloned.1.call-done) | copy-start | bytes 540676
Sparse Core Ops, SparseCore 0:
  141.0 62.7 all-reduce.3
  1908.5 269.4 all-reduce.5
  2186.1 64.7 all-reduce.7
Sparse Core Ops, SparseCore 1:
  143.8 774.6 all-gather.4
  920.7 980.9 all-gather.6
where the time goes:
time: 2260 us
  waiting for transfers between devices  2120 us (94%)
  other arithmetic  53 us (2%)
  starting transfers between devices  39.1 us (2%)
  local copies, waits for them, and re-layouts  24 us (1%)
    all_gather x1, waiting for transfers between devices, on_device(): lax.all_gather(down_weight, 'dp', axis=0, tiled=True)  980 us
    all_gather x1, waiting for transfers between devices, on_device(): lax.all_gather(up_weight, 'dp', axis=0, tiled=True)  713 us
    psum x1, waiting for transfers between devices, on_device(): lax.psum(round_term(branch).astype(jnp.bfloat16), 'seq').astype(jnp.float32)  270 us
    psum x1, waiting for transfers between devices, on_device(): lax.psum(round_term(slope_part).astype(jnp.bfloat16), 'seq')  63.5 us
    psum x1, waiting for transfers between devices, on_device(): lax.psum(partial_embed.astype(jnp.bfloat16), 'seq').astype(jnp.float32)  60.2 us
  transfers between devices with their start and end apart: 10, of which 10 were waited for; matrix products, arithmetic and copies ran while one was open for 2% of the time, Pallas kernels for 0%

commit v1 on v0

v1 whole, which is shorter than its diff:
```python
import jax
import jax.numpy as jnp
from jax import lax
from jax.experimental import pallas as pl
from jax.experimental.pallas import tpu as pltpu
from jax.sharding import Mesh, PartitionSpec as P


HEAD = 128
IMG, TXT, GROUPS = 64, 128, 4
ROWS = 3 * IMG + 2 * TXT
WIDTH = 384
EMB = 1408
HIDDEN = 768

epsilon = 1e-06
root_half = 0.7071067811865476
inv_root_tau = 0.3989422804014327
f32 = jnp.float32
bf16 = jnp.bfloat16


def pack_body(query, key, value, text_key, text_value, packed):
    for group in range(GROUPS):
        cols = pl.ds(group * WIDTH, WIDTH)
        packed[group, 0:64, :] = query[0, :, cols]
        packed[group, 64:128, :] = key[0, :, cols]
        packed[group, 128:256, :] = text_key[0, :, cols]
        packed[group, 256:320, :] = value[0, :, cols]
        packed[group, 320:448, :] = text_value[0, :, cols]


def norm_rows(rows, gain_row):
    rows = rows.astype(f32)
    inverse_rms = lax.rsqrt(jnp.mean(rows * rows, axis=-1, keepdims=True) + epsilon)
    return (rows * inverse_rms * gain_row).astype(bf16)


def matmul(left_side, right_side):
    return jnp.dot(left_side, right_side, preferred_element_type=f32)


def contract_rows(left_side, right_side):
    return lax.dot_general(left_side, right_side, (((1,), (1,)), ((), ())), preferred_element_type=f32)


def attend_body(packed, query_gain, key_gain, attended, pooled):
    for head in range(3):
        cols = slice(head * HEAD, (head + 1) * HEAD)
        query = jnp.concatenate([packed[s, 0:64, cols] for s in range(GROUPS)], axis=0)
        key = jnp.concatenate([packed[s, 64:256, cols] for s in range(GROUPS)], axis=0)
        value = jnp.concatenate([packed[s, 256:448, cols] for s in range(GROUPS)], axis=0)
        query = norm_rows(query, query_gain[...])
        key = norm_rows(key, key_gain[...])
        exponent = jnp.exp(contract_rows(query, key) * HEAD ** (-0.5))
        total = jnp.sum(exponent, axis=-1, keepdims=True)
        mixed = matmul(exponent.astype(bf16), value) / total
        attended[0, :, cols] = mixed.astype(bf16)
    reward_token = lax.broadcasted_iota(jnp.int32, (64, 256), 0)
    token = lax.broadcasted_iota(jnp.int32, (64, 256), 1)
    same_row = (token >> 6) == (reward_token >> 4)
    same_col = ((token & 31) >> 1) == (reward_token & 15)
    pool = jnp.where(same_row & same_col, 0.25, 0.0).astype(bf16)
    pooled[...] = matmul(pool, attended[0]).astype(bf16)


def layer_stats(residual):
    centered = residual - jnp.mean(residual, axis=-1, keepdims=True)
    inverse_std = lax.rsqrt(jnp.mean(centered * centered, axis=-1, keepdims=True) + epsilon)
    return (centered * inverse_std, inverse_std)


def layer_back(upstream, normed, inverse_std):
    return inverse_std * (
        upstream
        - jnp.mean(upstream, axis=-1, keepdims=True)
        - normed * jnp.mean(upstream * normed, axis=-1, keepdims=True)
    )


def embed_body(pooled, embed_weight, position_embed, residual_in):
    total = position_embed[...]
    for group in range(GROUPS):
        total = total + matmul(pooled[group], embed_weight[group * WIDTH : (group + 1) * WIDTH, :])
    residual_in[...] = total


def by_core(core, first, second, compute):
    @pl.when(core[0] == 0)
    def _():
        compute(first, second)

    @pl.when(core[0] != 0)
    def _():
        compute(second, first)


def forward_body(core, residual_in, norm_gain, first, second, branch, derivative_out, hidden):
    normed, _ = layer_stats(residual_in[...])
    hidden[...] = (normed * norm_gain[...]).astype(bf16)

    def compute(up, down):
        preact = contract_rows(hidden[...], up[...])
        cumulative = 0.5 * (1.0 + lax.erf(preact * root_half))
        derivative_out[...] = cumulative + preact * jnp.exp(-0.5 * preact * preact) * inv_root_tau
        part = matmul((preact * cumulative).astype(bf16), down[...]).astype(bf16)
        for group in range(GROUPS):
            branch[group] = part

    by_core(core, first, second, compute)


def sum_groups(parts):
    total = parts[0].astype(f32)
    for group in range(1, GROUPS):
        total = total + parts[group].astype(f32)
    return total


def backward_body(
    core, residual_in, branch, final_gain, reward_direction, derivative, first, second,
    slope, out_slope_out, reward,
):
    residual_out = residual_in[...] + sum_groups(branch)
    normed, inverse_std = layer_stats(residual_out)
    direction = final_gain[...] * reward_direction[...]
    reward[...] = jnp.full((8, 128), jnp.sum(normed * direction) * (1.0 / 64.0))
    out_slope_out[...] = layer_back(direction, normed, inverse_std)

    def compute(up, down):
        back_slope = contract_rows(out_slope_out[...].astype(bf16), down[...])
        hidden_slope = (back_slope * derivative[...]).astype(bf16)
        part = matmul(hidden_slope, up[...]).astype(bf16)
        for group in range(GROUPS):
            slope[group] = part

    by_core(core, first, second, compute)


def finish_body(group, residual_in, out_slope, slope, norm_gain, embed_weight, gradient):
    embed_rows = embed_weight[pl.ds(pl.multiple_of(group[0] * WIDTH, WIDTH), WIDTH), :]
    normed, inverse_std = layer_stats(residual_in[...])
    weighted = sum_groups(slope) * norm_gain[...]
    input_slope = out_slope[...] + layer_back(weighted, normed, inverse_std)
    pooled_slope = (0.25 * contract_rows(input_slope.astype(bf16), embed_rows)).astype(bf16)
    token = lax.broadcasted_iota(jnp.int32, (256, 64), 0)
    reward_token = lax.broadcasted_iota(jnp.int32, (256, 64), 1)
    same_row = (token >> 6) == (reward_token >> 4)
    same_col = ((token & 31) >> 1) == (reward_token & 15)
    spread = jnp.where(same_row & same_col, 1.0, 0.0).astype(bf16)
    gradient[0] = matmul(spread, pooled_slope).astype(bf16)


def shape(dims, dtype):
    return jax.ShapeDtypeStruct(dims, dtype)


def held(value):
    return pltpu.with_memory_space_constraint(value, pltpu.VMEM)


def in_hbm(value):
    return pltpu.with_memory_space_constraint(value, pltpu.HBM)


def in_vmem(count):
    return [pl.BlockSpec(memory_space=pltpu.VMEM)] * count


scalar_spec = pl.BlockSpec(memory_space=pltpu.SMEM)


def on_device(
    image_query, image_key, image_value, text_key, text_value, query_gain, key_gain, embed_weight,
    position_embed, norm_gain, final_gain, up_weight, down_weight, reward_direction,
):
    core = lax.axis_index("core").astype(jnp.int32).reshape(1)
    group = lax.axis_index("seq").astype(jnp.int32).reshape(1)
    nearby = lax.all_gather(
        jnp.concatenate([up_weight, down_weight], axis=0), ("zl", "core"), axis=0, tiled=False
    )
    nearby_up = nearby[:, 0:4, :].reshape(24, EMB)
    nearby_down = nearby[:, 4:8, :].reshape(24, EMB)
    mine = jnp.where(core[0] == 0, nearby_up, nearby_down)
    mine = lax.all_gather(mine, "x", axis=0, tiled=True)
    first = lax.all_gather(mine, "y", axis=0, tiled=True)
    second = lax.ppermute(first, "core", [(0, 1), (1, 0)])

    first, second = in_hbm(first), in_hbm(second)
    packed = pl.pallas_call(
        pack_body, out_shape=shape((GROUPS, ROWS, WIDTH), bf16), in_specs=in_vmem(5),
        out_specs=pl.BlockSpec(memory_space=pltpu.VMEM), name="pack",
    )(image_query, image_key, image_value, text_key, text_value)
    packed = lax.all_to_all(packed, "seq", split_axis=0, concat_axis=0, tiled=True)
    attended, pooled = pl.pallas_call(
        attend_body, out_shape=(shape((1, 256, WIDTH), bf16), shape((64, WIDTH), bf16)),
        in_specs=in_vmem(3), out_specs=tuple(in_vmem(2)), name="attend",
    )(held(packed), query_gain.reshape(1, HEAD), key_gain.reshape(1, HEAD))
    pooled = lax.all_gather(pooled, "seq", axis=0, tiled=False)
    residual_in = pl.pallas_call(
        embed_body, out_shape=shape((64, EMB), f32), in_specs=in_vmem(3),
        out_specs=pl.BlockSpec(memory_space=pltpu.VMEM), name="embed",
    )(pooled, embed_weight, position_embed)
    gain_row = norm_gain.reshape(1, EMB)
    branch, derivative = pl.pallas_call(
        forward_body, out_shape=(shape((GROUPS, 64, EMB), bf16), shape((64, HIDDEN), f32)),
        in_specs=[scalar_spec, *in_vmem(4)], out_specs=tuple(in_vmem(2)),
        scratch_shapes=[pltpu.VMEM((64, EMB), bf16)], name="forward",
    )(core, residual_in, gain_row, first, second)
    branch = lax.all_to_all(branch, "seq", split_axis=0, concat_axis=0, tiled=True)
    slope, out_slope, reward = pl.pallas_call(
        backward_body,
        out_shape=(shape((GROUPS, 64, EMB), bf16), shape((64, EMB), f32), shape((8, 128), f32)),
        in_specs=[scalar_spec, *in_vmem(7)], out_specs=tuple(in_vmem(3)), name="backward",
    )(
        core, residual_in, held(branch), final_gain.reshape(1, EMB), reward_direction.reshape(1, EMB),
        derivative, first, second,
    )
    slope = lax.all_to_all(slope, "seq", split_axis=0, concat_axis=0, tiled=True)
    gradient = pl.pallas_call(
        finish_body, out_shape=shape((1, 256, WIDTH), bf16),
        in_specs=[scalar_spec, *in_vmem(5)], out_specs=pl.BlockSpec(memory_space=pltpu.VMEM),
        name="finish",
    )(group, residual_in, out_slope, held(slope), gain_row, embed_weight)
    return (attended, gradient, reward[0, 0:1])


def solution(mesh):
    fine = Mesh(mesh.devices.reshape(4, 8, 3, 2, 4), ("x", "y", "zl", "core", "seq"))
    dp = ("x", "y", "zl", "core")
    return jax.shard_map(
        on_device,
        mesh=fine,
        in_specs=(
            P(dp, "seq", None),
            P(dp, "seq", None),
            P(dp, "seq", None),
            P(dp, "seq", None),
            P(dp, "seq", None),
            P(),
            P(),
            P(),
            P(),
            P(),
            P(),
            P((*dp, "seq"), None),
            P((*dp, "seq"), None),
            P(),
        ),
        out_specs=(P(dp, None, "seq"), P(dp, None, "seq"), P(dp)),
        check_vma=False,
    )
```

time: 2260 us -> 207 us (0.09)
  the two profiles are of different devices: /device:TPU:6 before, /device:TPU:32 now
where the time goes in v1:
time: 207 us
  waiting for transfers between devices  89.4 us (43%)
  blocking collectives  42.2 us (20%)
  starting transfers between devices  32.1 us (16%)
  Pallas kernels  23.6 us (11%)
  between operations  14.1 us (7%)
  local copies, waits for them, and re-layouts  4.34 us (2%)
    all_gather x1, waiting for transfers between devices, on_device(): first = lax.all_gather(mine, 'y', axis=0, tiled=True)  32 us
    all_to_all x1, waiting for transfers between devices, on_device(): lax.all_to_all(slope, 'seq', split_axis=0, concat_axis=0, tiled=True)  24.7 us
    all_to_all x1, waiting for transfers between devices, on_device(): lax.all_to_all(branch, 'seq', split_axis=0, concat_axis=0, tiled=True)  18.4 us
    all_gather x1, blocking collectives, on_device(): pooled = lax.all_gather(pooled, 'seq', axis=0, tiled=False)  16.9 us
    all_to_all x1, starting transfers between devices, on_device(): lax.all_to_all(packed, 'seq', split_axis=0, concat_axis=0, tiled=True)  14.5 us
    all_to_all x1, waiting for transfers between devices, on_device(): lax.all_to_all(packed, 'seq', split_axis=0, concat_axis=0, tiled=True)  14.3 us
    all_gather x1, blocking collectives, on_device(): mine = lax.all_gather(mine, 'x', axis=0, tiled=True)  13.4 us
    all_gather x1, blocking collectives, on_device(): lax.all_gather(jnp.concatenate([up_weight, down_weight], axis=0), ('zl',...  11.9 us
  transfers between devices with their start and end apart: 5, of which 4 were waited for; matrix products, arithmetic and copies ran while one was open for 1% of the time, Pallas kernels for 4%

profile of v1, /device:TPU:32, one launch (start us, length us, event | category | flops | bytes accessed | tf_op | source)
XLA Modules:
  0.0 206.5 jit_solution(11172133243699758155)
XLA Ops:
  7.2 0.0 all-gather.4.cloned.1.call-start
  7.2 0.7 pad_maximum_fusion
  8.0 11.9 %all-gather.1 = bf16[48,1408]{1,0:T(8,128)(2,1)S(1)} all-gather(bf16[8,1408]{1,0:T(8,128)(2,1)S(1)} %pad_maximum_fusion), channel_id=3, replica_groups=mesh['x'=4,'y'=8,'zl'=3,'core'=2,'seq'=4] {'zl','core'}, dimensions={0}, use_global_device_ids=true | all-gather | bytes 157696 | tf_op jit(solution)/shard_map/all_gather | solution.py:179
  19.9 0.1 slice_select_fusion
  20.0 13.4 %all_gather.22 = bf16[96,1408]{1,0:T(8,128)(2,1)} all-gather(bf16[24,1408]{1,0:T(8,128)(2,1)S(1)} %select_n.13), channel_id=1, replica_groups=mesh['x'=4,'y'=8,'zl'=3,'core'=2,'seq'=4] {'x'}, dimensions={0}, use_global_device_ids=true | all-gather | bytes 337920 | tf_op jit(solution)/shard_map/all_gather | solution.py:185
  33.4 0.0 all-gather.4.cloned.1.call-update
  33.4 0.0 copy-start.1
  33.4 2.5 %pack.1 = bf16[4,448,384]{2,1,0:T(8,128)(2,1)} custom-call(bf16[1,64,1536]{2,1,0:T(8,128)(2,1)} %query.1, bf16[1,64,1536]{2,1,0:T(8,128)(2,1)} %key.1, bf16[1,64,1536]{2,1,0:T(8,128)(2,1)} %value.1, bf16[1,128,1536]{2,1,0:T(8,128)(2,1)} %text_key.1, bf16[1,128,1536]{2,1,0:T(8,128)(2,1)} %text_value.1), custom_call_target="tpu_custom_call" | custom-call | tf_op jit(solution)/shard_map/pack/pallas_call | solution.py:190
  35.9 14.5 %all-to-all-start = ((bf16[4,448,384]{2,1,0:T(8,128)(2,1)}), bf16[4,448,384]{2,1,0:T(8,128)(2,1)S(1)}, u32[]{:S(2)}, u32[]{:S(2)}) async-start(bf16[4,448,384]{2,1,0:T(8,128)(2,1)} %pack.1), calls=%async_computation | async-start | bytes 2752512 | tf_op jit(solution)/shard_map/all_to_all | solution.py:194
  50.5 32.0 %all-gather.4.cloned.1.call-done.first = bf16[768,1408]{1,0:T(8,128)(2,1)} async-done(((bf16[96,1408]{1,0:T(8,128)(2,1)}), bf16[768,1408]{1,0:T(8,128)(2,1)}) %all-gather.4.cloned.1.call-update) | async-done | bytes 2162704 | tf_op jit(solution)/shard_map/all_gather | solution.py:186
  82.4 1.9 collective-permute-start
  84.3 0.0 copy-done.1
  84.3 0.6 reshape.35.norm_gain
  84.9 14.3 %all-to-all-done.packed = bf16[4,448,384]{2,1,0:T(8,128)(2,1)S(1)} async-done(((bf16[4,448,384]{2,1,0:T(8,128)(2,1)}), bf16[4,448,384]{2,1,0:T(8,128)(2,1)S(1)}, u32[]{:S(2)}, u32[]{:S(2)}) %all-to-all-start) | async-done | bytes 1376288 | tf_op jit(solution)/shard_map/all_to_all | solution.py:194
  99.2 2.6 %attend.1 = (bf16[1,256,384]{2,1,0:T(8,128)(2,1)}, bf16[64,384]{1,0:T(8,128)(2,1)}) custom-call(bf16[4,448,384]{2,1,0:T(8,128)(2,1)S(1)} %all-to-all-done.packed, f32[1,128]{1,0:T(1,128)} %bitcast.9, f32[1,128]{1,0:T(1,128)} %bitcast.10), custom_call_target="tpu_custom_call" | custom-call | tf_op jit(solution)/shard_map/attend/pallas_call | solution.py:195
  101.8 16.9 %all-gather = bf16[256,384]{1,0:T(8,128)(2,1)} all-gather(bf16[64,384]{1,0:T(8,128)(2,1)} %get-tuple-element.11), channel_id=2, replica_groups=mesh['x'=4,'y'=8,'zl'=3,'core'=2,'seq'=4] {'seq'}, dimensions={0}, use_global_device_ids=true | all-gather | bytes 245760 | tf_op jit(solution)/shard_map/all_gather | solution.py:199
  118.7 3.9 %embed.1.residual_in = f32[64,1408]{1,0:T(8,128)} custom-call(bf16[4,64,384]{2,1,0:T(8,128)(2,1)} %bitcast.7, bf16[1536,1408]{1,0:T(8,128)(2,1)} %embed_weight.3, f32[64,1408]{1,0:T(8,128)} %position_embed.1), custom_call_target="tpu_custom_call" | custom-call | tf_op jit(solution)/shard_map/embed/pallas_call | solution.py:200
  122.6 0.0 collective-permute-done.second
  122.6 0.0 copy-start
  122.6 1.3 copy-done
  123.9 0.0 copy-start.2
  123.9 0.0 copy-start.3
  123.9 5.0 %forward.1 = (bf16[4,64,1408]{2,1,0:T(8,128)(2,1)}, f32[64,768]{1,0:T(8,128)}) custom-call(s32[1]{0:T(128)} %bitcast.4.core, f32[64,1408]{1,0:T(8,128)} %embed.1.residual_in, f32[1,1408]{1,0:T(1,128)} %reshape.35.norm_gain, bf16[768,1408]{1,0:T(8,128)(2,1)} %all-gather.4.cloned.1.call-done.first, bf16[768,1408]{1,0:T(8,128)(2,1)} %copy-done), custom_call_target="tpu_custom_call" | custom-call | tf_op jit(solution)/shard_map/forward/pallas_call | solution.py:205
  128.9 5.8 %all-to-all-start.1 = ((bf16[4,64,1408]{2,1,0:T(8,128)(2,1)}), bf16[4,64,1408]{2,1,0:T(8,128)(2,1)S(1)}, u32[]{:S(2)}, u32[]{:S(2)}) async-start(bf16[4,64,1408]{2,1,0:T(8,128)(2,1)} %get-tuple-element.12), calls=%async_computation.1 | async-start | bytes 1441792 | tf_op jit(solution)/shard_map/all_to_all | solution.py:210
  134.8 0.0 copy-done.2
  134.8 0.6 reshape.36.final_gain
  135.4 0.0 copy-done.3
  135.4 0.6 reshape.37.reward_direction
  136.0 18.4 %all-to-all-done.1.branch = bf16[4,64,1408]{2,1,0:T(8,128)(2,1)S(1)} async-done(((bf16[4,64,1408]{2,1,0:T(8,128)(2,1)}), bf16[4,64,1408]{2,1,0:T(8,128)(2,1)S(1)}, u32[]{:S(2)}, u32[]{:S(2)}) %all-to-all-start.1) | async-done | bytes 720928 | tf_op jit(solution)/shard_map/all_to_all | solution.py:210
  154.4 5.4 %backward.1 = (bf16[4,64,1408]{2,1,0:T(8,128)(2,1)}, f32[64,1408]{1,0:T(8,128)}, f32[8,128]{1,0:T(8,128)}) custom-call(s32[1]{0:T(128)} %bitcast.4.core, f32[64,1408]{1,0:T(8,128)} %embed.1.residual_in, bf16[4,64,1408]{2,1,0:T(8,128)(2,1)S(1)} %all-to-all-done.1.branch, f32[1,1408]{1,0:T(1,128)} %reshape.36.final_gain, f32[1,1408]{1,0:T(1,128)} %reshape.37.reward_direction, ...), custom_call_target="tpu_custom_call" | custom-call | tf_op jit(solution)/shard_map/backward/pallas_call | solution.py:211
  159.8 9.8 %all-to-all-start.2 = ((bf16[4,64,1408]{2,1,0:T(8,128)(2,1)}), bf16[4,64,1408]{2,1,0:T(8,128)(2,1)S(1)}, u32[]{:S(2)}, u32[]{:S(2)}) async-start(bf16[4,64,1408]{2,1,0:T(8,128)(2,1)} %get-tuple-element.15), calls=%async_computation.2 | async-start | bytes 1441792 | tf_op jit(solution)/shard_map/all_to_all | solution.py:219
  169.6 1.2 slice.11
  170.8 24.7 %all-to-all-done.2.slope = bf16[4,64,1408]{2,1,0:T(8,128)(2,1)S(1)} async-done(((bf16[4,64,1408]{2,1,0:T(8,128)(2,1)}), bf16[4,64,1408]{2,1,0:T(8,128)(2,1)S(1)}, u32[]{:S(2)}, u32[]{:S(2)}) %all-to-all-start.2) | async-done | bytes 720928 | tf_op jit(solution)/shard_map/all_to_all | solution.py:219
  195.5 4.2 %finish.1 = bf16[1,256,384]{2,1,0:T(8,128)(2,1)} custom-call(s32[1]{0:T(128)} %bitcast.2.group, f32[64,1408]{1,0:T(8,128)} %embed.1.residual_in, f32[64,1408]{1,0:T(8,128)} %get-tuple-element.14.out_slope, bf16[4,64,1408]{2,1,0:T(8,128)(2,1)S(1)} %all-to-all-done.2.slope, f32[1,1408]{1,0:T(1,128)} %reshape.35.norm_gain, bf16[1536,1408]{1,0:T(8,128)(2,1)} %embed_weight.3), custom_call_target="tpu_custom_call" | custom-call | tf_op jit(solution)/shard_map/finish/pallas_call | solution.py:220
  (1 shorter events, 0.0 us)
Async XLA Ops:
  7.2 75.3 %all-gather.4.cloned.1.call-start = ((), (), s32[]{:S(2)}) async-start(), calls=%async_computation.3 | async-start | bytes 2433024 | tf_op jit(solution)/shard_map/all_gather | solution.py:186
  33.4 51.0 %copy-start.1 = (f32[1408]{0:T(1024)S(1)}, f32[1408]{0:T(1024)}, u32[]{:S(2)}) copy-start(f32[1408]{0:T(1024)} %param.23) | copy-start | bytes 16900
  35.9 63.3 %all-to-all-start = ((bf16[4,448,384]{2,1,0:T(8,128)(2,1)}), bf16[4,448,384]{2,1,0:T(8,128)(2,1)S(1)}, u32[]{:S(2)}, u32[]{:S(2)}) async-start(bf16[4,448,384]{2,1,0:T(8,128)(2,1)} %pack.1), calls=%async_computation | async-start | bytes 2752512 | tf_op jit(solution)/shard_map/all_to_all | solution.py:194
  82.4 40.1 %collective-permute-start = (bf16[768,1408]{1,0:T(8,128)(2,1)}, bf16[768,1408]{1,0:T(8,128)(2,1)S(1)}, u32[]{:S(2)}, u32[]{:S(2)}) collective-permute-start(bf16[768,1408]{1,0:T(8,128)(2,1)} %all-gather.4.cloned.1.call-done.first), channel_id=1, source_target_pairs={{0,4},{4,0},{1,5},{5,1},{2,6},{6,2},{3,7},{7,3},{8,12},{12,8},{9,1... | collective-permute-start | bytes 6488072 | tf_op jit(solution)/shard_map/ppermute | solution.py:187
  122.6 1.3 copy-start
  123.9 10.9 %copy-start.2 = (f32[1408]{0:T(1024)S(1)}, f32[1408]{0:T(1024)}, u32[]{:S(2)}) copy-start(f32[1408]{0:T(1024)} %param.24) | copy-start | bytes 16900
  123.9 11.5 %copy-start.3 = (f32[1408]{0:T(1024)S(1)}, f32[1408]{0:T(1024)}, u32[]{:S(2)}) copy-start(f32[1408]{0:T(1024)} %param.27) | copy-start | bytes 16900
  128.9 25.4 %all-to-all-start.1 = ((bf16[4,64,1408]{2,1,0:T(8,128)(2,1)}), bf16[4,64,1408]{2,1,0:T(8,128)(2,1)S(1)}, u32[]{:S(2)}, u32[]{:S(2)}) async-start(bf16[4,64,1408]{2,1,0:T(8,128)(2,1)} %get-tuple-element.12), calls=%async_computation.1 | async-start | bytes 1441792 | tf_op jit(solution)/shard_map/all_to_all | solution.py:210
  159.8 35.7 %all-to-all-start.2 = ((bf16[4,64,1408]{2,1,0:T(8,128)(2,1)}), bf16[4,64,1408]{2,1,0:T(8,128)(2,1)S(1)}, u32[]{:S(2)}, u32[]{:S(2)}) async-start(bf16[4,64,1408]{2,1,0:T(8,128)(2,1)} %get-tuple-element.15), calls=%async_computation.2 | async-start | bytes 1441792 | tf_op jit(solution)/shard_map/all_to_all | solution.py:219
Sparse Core Ops, SparseCore 0:
  33.5 48.8 all-gather.3

commit v2 on v1

--- a/solution.py
+++ b/solution.py
@@ -13,6 +13,7 @@
 EMB = 1408
 HIDDEN = 768
 
+
 epsilon = 1e-06
 root_half = 0.7071067811865476
 inv_root_tau = 0.3989422804014327
@@ -20,14 +21,15 @@
 bf16 = jnp.bfloat16
 
 
-def pack_body(query, key, value, text_key, text_value, packed):
-    for group in range(GROUPS):
-        cols = pl.ds(group * WIDTH, WIDTH)
-        packed[group, 0:64, :] = query[0, :, cols]
-        packed[group, 64:128, :] = key[0, :, cols]
-        packed[group, 128:256, :] = text_key[0, :, cols]
-        packed[group, 256:320, :] = value[0, :, cols]
-        packed[group, 320:448, :] = text_value[0, :, cols]
+def pack_body(place, query, key, value, text_key, text_value, *packed):
+    for step in range(GROUPS):
+        group = (place[0] + step) % GROUPS
+        cols = pl.ds(pl.multiple_of(group * WIDTH, HEAD), WIDTH)
+        packed[step][0:64, :] = query[0, :, cols]
+        packed[step][64:128, :] = key[0, :, cols]
+        packed[step][128:256, :] = text_key[0, :, cols]
+        packed[step][256:320, :] = value[0, :, cols]
+        packed[step][320:448, :] = text_value[0, :, cols]
 
 
 def norm_rows(rows, gain_row):
@@ -44,18 +46,22 @@
     return lax.dot_general(left_side, right_side, (((1,), (1,)), ((), ())), preferred_element_type=f32)
 
 
-def attend_body(packed, query_gain, key_gain, attended, pooled):
+def attend_body(place, first, second, third, fourth, query_gain, key_gain, attended, pooled):
+    packed = (first, second, third, fourth)
     for head in range(3):
         cols = slice(head * HEAD, (head + 1) * HEAD)
-        query = jnp.concatenate([packed[s, 0:64, cols] for s in range(GROUPS)], axis=0)
-        key = jnp.concatenate([packed[s, 64:256, cols] for s in range(GROUPS)], axis=0)
-        value = jnp.concatenate([packed[s, 256:448, cols] for s in range(GROUPS)], axis=0)
+        query = jnp.concatenate([packed[s][0:64, cols] for s in range(GROUPS)], axis=0)
+        key = jnp.concatenate([packed[s][64:256, cols] for s in range(GROUPS)], axis=0)
+        value = jnp.concatenate([packed[s][256:448, cols] for s in range(GROUPS)], axis=0)
         query = norm_rows(query, query_gain[...])
         key = norm_rows(key, key_gain[...])
         exponent = jnp.exp(contract_rows(query, key) * HEAD ** (-0.5))
         total = jnp.sum(exponent, axis=-1, keepdims=True)
         mixed = matmul(exponent.astype(bf16), value) / total
-        attended[0, :, cols] = mixed.astype(bf16)
+        for step in range(GROUPS):
+            source = (place[0] + GROUPS - step) % GROUPS
+            rows = pl.ds(pl.multiple_of(source * IMG, IMG), IMG)
+            attended[0, rows, cols] = mixed[step * IMG : (step + 1) * IMG].astype(bf16)
     reward_token = lax.broadcasted_iota(jnp.int32, (64, 256), 0)
     token = lax.broadcasted_iota(jnp.int32, (64, 256), 1)
     same_row = (token >> 6) == (reward_token >> 4)
@@ -170,32 +176,39 @@
 scalar_spec = pl.BlockSpec(memory_space=pltpu.SMEM)
 
 
+def spread_to(value, axes, count):
+    copies = jnp.broadcast_to(value[None], (count, *value.shape))
+    return lax.all_to_all(copies, axes, split_axis=0, concat_axis=0, tiled=True)
+
+
 def on_device(
     image_query, image_key, image_value, text_key, text_value, query_gain, key_gain, embed_weight,
     position_embed, norm_gain, final_gain, up_weight, down_weight, reward_direction,
 ):
     core = lax.axis_index("core").astype(jnp.int32).reshape(1)
     group = lax.axis_index("seq").astype(jnp.int32).reshape(1)
-    nearby = lax.all_gather(
-        jnp.concatenate([up_weight, down_weight], axis=0), ("zl", "core"), axis=0, tiled=False
-    )
+    nearby = spread_to(jnp.concatenate([up_weight, down_weight], axis=0), ("zl", "core"), 6)
     nearby_up = nearby[:, 0:4, :].reshape(24, EMB)
     nearby_down = nearby[:, 4:8, :].reshape(24, EMB)
     mine = jnp.where(core[0] == 0, nearby_up, nearby_down)
     mine = lax.all_gather(mine, "x", axis=0, tiled=True)
-    first = lax.all_gather(mine, "y", axis=0, tiled=True)
+    first = spread_to(mine, "y", 8).reshape(HIDDEN, EMB)
     second = lax.ppermute(first, "core", [(0, 1), (1, 0)])
 
     first, second = in_hbm(first), in_hbm(second)
     packed = pl.pallas_call(
-        pack_body, out_shape=shape((GROUPS, ROWS, WIDTH), bf16), in_specs=in_vmem(5),
-        out_specs=pl.BlockSpec(memory_space=pltpu.VMEM), name="pack",
-    )(image_query, image_key, image_value, text_key, text_value)
-    packed = lax.all_to_all(packed, "seq", split_axis=0, concat_axis=0, tiled=True)
+        pack_body, out_shape=(shape((ROWS, WIDTH), bf16),) * GROUPS, in_specs=[scalar_spec, *in_vmem(5)],
+        out_specs=tuple(in_vmem(GROUPS)), name="pack",
+    )(group, image_query, image_key, image_value, text_key, text_value)
+    received = [packed[0]]
+    for step in (2, 1, 3):
+        around = [(member, (member + step) % GROUPS) for member in range(GROUPS)]
+        received.append(lax.ppermute(packed[step], "seq", around))
+    received = [received[0], received[2], received[1], received[3]]
     attended, pooled = pl.pallas_call(
         attend_body, out_shape=(shape((1, 256, WIDTH), bf16), shape((64, WIDTH), bf16)),
-        in_specs=in_vmem(3), out_specs=tuple(in_vmem(2)), name="attend",
-    )(held(packed), query_gain.reshape(1, HEAD), key_gain.reshape(1, HEAD))
+        in_specs=[scalar_spec, *in_vmem(6)], out_specs=tuple(in_vmem(2)), name="attend",
+    )(group, *map(held, received), query_gain.reshape(1, HEAD), key_gain.reshape(1, HEAD))
     pooled = lax.all_gather(pooled, "seq", axis=0, tiled=False)
     residual_in = pl.pallas_call(
         embed_body, out_shape=shape((64, EMB), f32), in_specs=in_vmem(3),

time: 207 us -> 250 us (1.21)
  the two profiles are of different devices: /device:TPU:32 before, /device:TPU:4 now
where the time goes in v2:
time: 250 us; the launch traced here: 249 us
  blocking collectives  89.6 us (36%)
  waiting for transfers between devices  87.8 us (35%)
  starting transfers between devices  41.6 us (17%)
  Pallas kernels  23.7 us (9%)
  local copies, waits for them, and re-layouts  4.81 us (2%)
    all_to_all x1, blocking collectives, spread_to(): return lax.all_to_all(copies, axes, split_axis=0, concat_axis=0, tiled=True)  52.7 us
    ppermute x3, waiting for transfers between devices, on_device(): received.append(lax.ppermute(packed[step], 'seq', around))  40.4 us
    ppermute x3, starting transfers between devices, on_device(): received.append(lax.ppermute(packed[step], 'seq', around))  21.3 us
    all_to_all x1, waiting for transfers between devices, on_device(): lax.all_to_all(slope, 'seq', split_axis=0, concat_axis=0, tiled=True)  21.2 us
    all_to_all x1, waiting for transfers between devices, on_device(): lax.all_to_all(branch, 'seq', split_axis=0, concat_axis=0, tiled=True)  20.1 us
    all_gather x1, blocking collectives, on_device(): pooled = lax.all_gather(pooled, 'seq', axis=0, tiled=False)  19.3 us
    all_gather x1, blocking collectives, on_device(): mine = lax.all_gather(mine, 'x', axis=0, tiled=True)  17.6 us
    all_to_all x1, starting transfers between devices, on_device(): lax.all_to_all(slope, 'seq', split_axis=0, concat_axis=0, tiled=True)  7.16 us
  transfers between devices with their start and end apart: 7, of which 6 were waited for; matrix products, arithmetic and copies ran while one was open for 1% of the time, Pallas kernels for 4%

profile of v2, /device:TPU:4, one launch (start us, length us, event | category | flops | bytes accessed | tf_op | source)
XLA Modules:
  0.0 249.0 jit_solution(587154085232871528)
XLA Ops:
  0.6 0.7 pad_maximum_fusion
  1.4 0.7 broadcast_in_dim.4
  2.0 5.5 %all-to-all-start = ((bf16[6,8,1408]{2,1,0:T(8,128)(2,1)}), bf16[6,8,1408]{2,1,0:T(8,128)(2,1)S(1)}, u32[]{:S(2)}, u32[]{:S(2)}) async-start(bf16[6,8,1408]{2,1,0:T(8,128)(2,1)} %broadcast_in_dim.4), calls=%async_computation | async-start | bytes 270336 | tf_op jit(solution)/shard_map/all_to_all | solution.py:181
  7.5 6.0 %all-to-all-done = bf16[6,8,1408]{2,1,0:T(8,128)(2,1)S(1)} async-done(((bf16[6,8,1408]{2,1,0:T(8,128)(2,1)}), bf16[6,8,1408]{2,1,0:T(8,128)(2,1)S(1)}, u32[]{:S(2)}, u32[]{:S(2)}) %all-to-all-start) | async-done | bytes 135200 | tf_op jit(solution)/shard_map/all_to_all | solution.py:181
  13.5 0.1 slice_select_fusion
  13.6 17.6 %all_gather.11 = bf16[96,1408]{1,0:T(8,128)(2,1)S(1)} all-gather(bf16[24,1408]{1,0:T(8,128)(2,1)S(1)} %select_n.13), channel_id=1, replica_groups=mesh['x'=4,'y'=8,'zl'=3,'core'=2,'seq'=4] {'x'}, dimensions={0}, use_global_device_ids=true | all-gather | bytes 337920 | tf_op jit(solution)/shard_map/all_gather | solution.py:194
  31.2 0.2 broadcast_in_dim.5
  31.3 0.0 copy-start.1
  31.4 52.7 %all_to_all.20 = bf16[8,96,1408]{2,1,0:T(8,128)(2,1)} all-to-all(bf16[8,96,1408]{2,1,0:T(8,128)(2,1)S(1)} %broadcast_in_dim.5), channel_id=1, replica_groups=mesh['x'=4,'y'=8,'zl'=3,'core'=2,'seq'=4] {'y'}, dimensions={0} | all-to-all | bytes 4325376 | tf_op jit(solution)/shard_map/all_to_all | solution.py:181
  84.0 1.9 collective-permute-start.3
  85.9 2.6 %pack.1 = (bf16[448,384]{1,0:T(8,128)(2,1)}, bf16[448,384]{1,0:T(8,128)(2,1)}, bf16[448,384]{1,0:T(8,128)(2,1)}, bf16[448,384]{1,0:T(8,128)(2,1)}) custom-call(s32[1]{0:T(128)} %bitcast.place.group, bf16[1,64,1536]{2,1,0:T(8,128)(2,1)} %query.1, bf16[1,64,1536]{2,1,0:T(8,128)(2,1)} %key.1, bf16[1,64,1536]{2,1,0:T(8,128)(2,1)} %value.1, ...), custom_call_target="tpu_custom_call" | custom-call | tf_op jit(solution)/shard_map/pack/pallas_call | solution.py:199
  88.5 8.2 %collective-permute-start = (bf16[448,384]{1,0:T(8,128)(2,1)}, bf16[448,384]{1,0:T(8,128)(2,1)S(1)}, u32[]{:S(2)}, u32[]{:S(2)}) collective-permute-start(bf16[448,384]{1,0:T(8,128)(2,1)} %get-tuple-element.15), channel_id=1, source_target_pairs={{0,1},{1,2},{2,3},{3,0},{4,5},{5,6},{6,7},{7,4},{8,9},{9,10},{10,1... | collective-permute-start | bytes 1032200 | tf_op jit(solution)/shard_map/ppermute | solution.py:206
  96.8 8.8 %collective-permute-start.1 = (bf16[448,384]{1,0:T(8,128)(2,1)}, bf16[448,384]{1,0:T(8,128)(2,1)S(1)}, u32[]{:S(2)}, u32[]{:S(2)}) collective-permute-start(bf16[448,384]{1,0:T(8,128)(2,1)} %get-tuple-element.16), channel_id=1, source_target_pairs={{0,2},{1,3},{2,0},{3,1},{4,6},{5,7},{6,4},{7,5},{8,10},{9,11},{10,... | collective-permute-start | bytes 1032200 | tf_op jit(solution)/shard_map/ppermute | solution.py:206
  105.6 4.3 %collective-permute-start.2 = (bf16[448,384]{1,0:T(8,128)(2,1)}, bf16[448,384]{1,0:T(8,128)(2,1)S(1)}, u32[]{:S(2)}, u32[]{:S(2)}) collective-permute-start(bf16[448,384]{1,0:T(8,128)(2,1)} %get-tuple-element.17), channel_id=1, source_target_pairs={{0,3},{1,0},{2,1},{3,2},{4,7},{5,4},{6,5},{7,6},{8,11},{9,8},{10,9... | collective-permute-start | bytes 1032200 | tf_op jit(solution)/shard_map/ppermute | solution.py:206
  109.9 0.0 copy-done.1
  109.9 0.6 reshape.40.norm_gain
  110.5 23.0 %collective-permute-done.second = bf16[448,384]{1,0:T(8,128)(2,1)S(1)} collective-permute-done((bf16[448,384]{1,0:T(8,128)(2,1)}, bf16[448,384]{1,0:T(8,128)(2,1)S(1)}, u32[]{:S(2)}, u32[]{:S(2)}) %collective-permute-start) | collective-permute-done | bytes 344096 | tf_op jit(solution)/shard_map/ppermute | solution.py:206
  133.5 15.1 %collective-permute-done.1.third = bf16[448,384]{1,0:T(8,128)(2,1)S(1)} collective-permute-done((bf16[448,384]{1,0:T(8,128)(2,1)}, bf16[448,384]{1,0:T(8,128)(2,1)S(1)}, u32[]{:S(2)}, u32[]{:S(2)}) %collective-permute-start.1) | collective-permute-done | bytes 344096 | tf_op jit(solution)/shard_map/ppermute | solution.py:206
  148.6 2.3 collective-permute-done.2.fourth
  150.9 0.0 copy-start
  150.9 1.0 copy-done
  151.9 2.6 %attend.1 = (bf16[1,256,384]{2,1,0:T(8,128)(2,1)}, bf16[64,384]{1,0:T(8,128)(2,1)}) custom-call(s32[1]{0:T(128)} %bitcast.place.group, bf16[448,384]{1,0:T(8,128)(2,1)S(1)} %copy-done, bf16[448,384]{1,0:T(8,128)(2,1)S(1)} %collective-permute-done.second, bf16[448,384]{1,0:T(8,128)(2,1)S(1)} %collective-permute-done.1.third, ...), custom_call_target="tpu_custom_call" | custom-call | tf_op jit(solution)/shard_map/attend/pallas_call | solution.py:208
  154.4 19.3 %all-gather = bf16[256,384]{1,0:T(8,128)(2,1)} all-gather(bf16[64,384]{1,0:T(8,128)(2,1)} %get-tuple-element.19), channel_id=2, replica_groups=mesh['x'=4,'y'=8,'zl'=3,'core'=2,'seq'=4] {'seq'}, dimensions={0}, use_global_device_ids=true | all-gather | bytes 245760 | tf_op jit(solution)/shard_map/all_gather | solution.py:212
  173.8 3.9 %embed.1.residual_in = f32[64,1408]{1,0:T(8,128)} custom-call(bf16[4,64,384]{2,1,0:T(8,128)(2,1)} %bitcast.7, bf16[1536,1408]{1,0:T(8,128)(2,1)} %embed_weight.3, f32[64,1408]{1,0:T(8,128)} %position_embed.1), custom_call_target="tpu_custom_call" | custom-call | tf_op jit(solution)/shard_map/embed/pallas_call | solution.py:213
  177.6 0.0 collective-permute-done.3.second
  177.6 0.0 copy-start.2
  177.7 0.0 copy-start.3
  177.7 5.0 %forward.1 = (bf16[4,64,1408]{2,1,0:T(8,128)(2,1)}, f32[64,768]{1,0:T(8,128)}) custom-call(s32[1]{0:T(128)} %bitcast.4.core, f32[64,1408]{1,0:T(8,128)} %embed.1.residual_in, f32[1,1408]{1,0:T(1,128)} %reshape.40.norm_gain, bf16[768,1408]{1,0:T(8,128)(2,1)} %bitcast.5.first, bf16[768,1408]{1,0:T(8,128)(2,1)} %collective-permute-done.3.second), custom_call_target="tpu_custom_call" | custom-call | tf_op jit(solution)/shard_map/forward/pallas_call | solution.py:218
  182.7 5.8 %all-to-all-start.2 = ((bf16[4,64,1408]{2,1,0:T(8,128)(2,1)}), bf16[4,64,1408]{2,1,0:T(8,128)(2,1)S(1)}, u32[]{:S(2)}, u32[]{:S(2)}) async-start(bf16[4,64,1408]{2,1,0:T(8,128)(2,1)} %get-tuple-element.20), calls=%async_computation.2 | async-start | bytes 1441792 | tf_op jit(solution)/shard_map/all_to_all | solution.py:223
  188.5 0.0 copy-done.2
  188.5 0.6 reshape.42.final_gain
  189.1 0.0 copy-done.3
  189.1 0.6 reshape.43.reward_direction
  189.7 20.1 %all-to-all-done.2.branch = bf16[4,64,1408]{2,1,0:T(8,128)(2,1)S(1)} async-done(((bf16[4,64,1408]{2,1,0:T(8,128)(2,1)}), bf16[4,64,1408]{2,1,0:T(8,128)(2,1)S(1)}, u32[]{:S(2)}, u32[]{:S(2)}) %all-to-all-start.2) | async-done | bytes 720928 | tf_op jit(solution)/shard_map/all_to_all | solution.py:223
  209.8 5.4 %backward.1 = (bf16[4,64,1408]{2,1,0:T(8,128)(2,1)}, f32[64,1408]{1,0:T(8,128)}, f32[8,128]{1,0:T(8,128)}) custom-call(s32[1]{0:T(128)} %bitcast.4.core, f32[64,1408]{1,0:T(8,128)} %embed.1.residual_in, bf16[4,64,1408]{2,1,0:T(8,128)(2,1)S(1)} %all-to-all-done.2.branch, f32[1,1408]{1,0:T(1,128)} %reshape.42.final_gain, f32[1,1408]{1,0:T(1,128)} %reshape.43.reward_direction, ...), custom_call_target="tpu_custom_call" | custom-call | tf_op jit(solution)/shard_map/backward/pallas_call | solution.py:224
  215.2 7.2 %all-to-all-start.3 = ((bf16[4,64,1408]{2,1,0:T(8,128)(2,1)}), bf16[4,64,1408]{2,1,0:T(8,128)(2,1)S(1)}, u32[]{:S(2)}, u32[]{:S(2)}) async-start(bf16[4,64,1408]{2,1,0:T(8,128)(2,1)} %get-tuple-element.23), calls=%async_computation.3 | async-start | bytes 1441792 | tf_op jit(solution)/shard_map/all_to_all | solution.py:232
  222.4 1.2 slice.11
  223.6 21.2 %all-to-all-done.3.slope = bf16[4,64,1408]{2,1,0:T(8,128)(2,1)S(1)} async-done(((bf16[4,64,1408]{2,1,0:T(8,128)(2,1)}), bf16[4,64,1408]{2,1,0:T(8,128)(2,1)S(1)}, u32[]{:S(2)}, u32[]{:S(2)}) %all-to-all-start.3) | async-done | bytes 720928 | tf_op jit(solution)/shard_map/all_to_all | solution.py:232
  244.8 4.2 %finish.1 = bf16[1,256,384]{2,1,0:T(8,128)(2,1)} custom-call(s32[1]{0:T(128)} %bitcast.place.group, f32[64,1408]{1,0:T(8,128)} %embed.1.residual_in, f32[64,1408]{1,0:T(8,128)} %get-tuple-element.22.out_slope, bf16[4,64,1408]{2,1,0:T(8,128)(2,1)S(1)} %all-to-all-done.3.slope, f32[1,1408]{1,0:T(1,128)} %reshape.40.norm_gain, bf16[1536,1408]{1,0:T(8,128)(2,1)} %embed_weight.3), custom_call_target="tpu_custom_call" | custom-call | tf_op jit(solution)/shard_map/finish/pallas_call | solution.py:233
  (1 shorter events, 0.0 us)
Async XLA Ops:
  2.0 11.5 %all-to-all-start = ((bf16[6,8,1408]{2,1,0:T(8,128)(2,1)}), bf16[6,8,1408]{2,1,0:T(8,128)(2,1)S(1)}, u32[]{:S(2)}, u32[]{:S(2)}) async-start(bf16[6,8,1408]{2,1,0:T(8,128)(2,1)} %broadcast_in_dim.4), calls=%async_computation | async-start | bytes 270336 | tf_op jit(solution)/shard_map/all_to_all | solution.py:181
  31.3 78.5 %copy-start.1 = (f32[1408]{0:T(1024)S(1)}, f32[1408]{0:T(1024)}, u32[]{:S(2)}) copy-start(f32[1408]{0:T(1024)} %param.23) | copy-start | bytes 16900
  84.0 93.6 %collective-permute-start.3 = (bf16[768,1408]{1,0:T(8,128)(2,1)}, bf16[768,1408]{1,0:T(8,128)(2,1)}, u32[]{:S(2)}, u32[]{:S(2)}) collective-permute-start(bf16[768,1408]{1,0:T(8,128)(2,1)} %bitcast.5.first), channel_id=1, source_target_pairs={{0,4},{4,0},{1,5},{5,1},{2,6},{6,2},{3,7},{7,3},{8,12},{12,8},{9,1... | collective-permute-start | bytes 6488072 | tf_op jit(solution)/shard_map/ppermute | solution.py:196
  88.5 45.0 %collective-permute-start = (bf16[448,384]{1,0:T(8,128)(2,1)}, bf16[448,384]{1,0:T(8,128)(2,1)S(1)}, u32[]{:S(2)}, u32[]{:S(2)}) collective-permute-start(bf16[448,384]{1,0:T(8,128)(2,1)} %get-tuple-element.15), channel_id=1, source_target_pairs={{0,1},{1,2},{2,3},{3,0},{4,5},{5,6},{6,7},{7,4},{8,9},{9,10},{10,1... | collective-permute-start | bytes 1032200 | tf_op jit(solution)/shard_map/ppermute | solution.py:206
  96.8 51.9 %collective-permute-start.1 = (bf16[448,384]{1,0:T(8,128)(2,1)}, bf16[448,384]{1,0:T(8,128)(2,1)S(1)}, u32[]{:S(2)}, u32[]{:S(2)}) collective-permute-start(bf16[448,384]{1,0:T(8,128)(2,1)} %get-tuple-element.16), channel_id=1, source_target_pairs={{0,2},{1,3},{2,0},{3,1},{4,6},{5,7},{6,4},{7,5},{8,10},{9,11},{10,... | collective-permute-start | bytes 1032200 | tf_op jit(solution)/shard_map/ppermute | solution.py:206
  105.6 45.3 %collective-permute-start.2 = (bf16[448,384]{1,0:T(8,128)(2,1)}, bf16[448,384]{1,0:T(8,128)(2,1)S(1)}, u32[]{:S(2)}, u32[]{:S(2)}) collective-permute-start(bf16[448,384]{1,0:T(8,128)(2,1)} %get-tuple-element.17), channel_id=1, source_target_pairs={{0,3},{1,0},{2,1},{3,2},{4,7},{5,4},{6,5},{7,6},{8,11},{9,8},{10,9... | collective-permute-start | bytes 1032200 | tf_op jit(solution)/shard_map/ppermute | solution.py:206
  150.9 1.0 copy-start
  177.6 10.8 %copy-start.2 = (f32[1408]{0:T(1024)S(1)}, f32[1408]{0:T(1024)}, u32[]{:S(2)}) copy-start(f32[1408]{0:T(1024)} %param.24) | copy-start | bytes 16900
  177.7 11.4 %copy-start.3 = (f32[1408]{0:T(1024)S(1)}, f32[1408]{0:T(1024)}, u32[]{:S(2)}) copy-start(f32[1408]{0:T(1024)} %param.27) | copy-start | bytes 16900
  182.7 27.1 %all-to-all-start.2 = ((bf16[4,64,1408]{2,1,0:T(8,128)(2,1)}), bf16[4,64,1408]{2,1,0:T(8,128)(2,1)S(1)}, u32[]{:S(2)}, u32[]{:S(2)}) async-start(bf16[4,64,1408]{2,1,0:T(8,128)(2,1)} %get-tuple-element.20), calls=%async_computation.2 | async-start | bytes 1441792 | tf_op jit(solution)/shard_map/all_to_all | solution.py:223
  215.2 29.6 %all-to-all-start.3 = ((bf16[4,64,1408]{2,1,0:T(8,128)(2,1)}), bf16[4,64,1408]{2,1,0:T(8,128)(2,1)S(1)}, u32[]{:S(2)}, u32[]{:S(2)}) async-start(bf16[4,64,1408]{2,1,0:T(8,128)(2,1)} %get-tuple-element.23), calls=%async_computation.3 | async-start | bytes 1441792 | tf_op jit(solution)/shard_map/all_to_all | solution.py:232

commit v3 on v2

--- a/solution.py
+++ b/solution.py
@@ -101,7 +101,7 @@
         compute(second, first)
 
 
-def forward_body(core, residual_in, norm_gain, first, second, branch, derivative_out, hidden):
+def forward_body(core, residual_in, norm_gain, first, second, low, high, derivative_out, hidden):
     normed, _ = layer_stats(residual_in[...])
     hidden[...] = (normed * norm_gain[...]).astype(bf16)
 
@@ -110,24 +110,37 @@
         cumulative = 0.5 * (1.0 + lax.erf(preact * root_half))
         derivative_out[...] = cumulative + preact * jnp.exp(-0.5 * preact * preact) * inv_root_tau
         part = matmul((preact * cumulative).astype(bf16), down[...]).astype(bf16)
-        for group in range(GROUPS):
-            branch[group] = part
+        low[...] = part[0:32]
+        high[...] = part[32:64]
 
     by_core(core, first, second, compute)
 
 
-def sum_groups(parts):
-    total = parts[0].astype(f32)
-    for group in range(1, GROUPS):
-        total = total + parts[group].astype(f32)
-    return total
+def sum_halves(halves):
+    low, low_other, high, high_other = halves
+    low = low[...].astype(f32) + low_other[...].astype(f32)
+    high = high[...].astype(f32) + high_other[...].astype(f32)
+    return jnp.concatenate([low, high], axis=0)
+
+
+def group_sum(low, high):
+    inner = [(0, 1), (1, 0), (2, 3), (3, 2)]
+    outer = [(0, 3), (3, 0), (1, 2), (2, 1)]
+
+    def pair_sum(mine, other):
+        return (mine.astype(f32) + other.astype(f32)).astype(bf16)
+
+    low_pair = lax.ppermute(low, "seq", inner)
+    high_pair = lax.ppermute(high, "seq", outer)
+    low, high = pair_sum(low, low_pair), pair_sum(high, high_pair)
+    return (low, lax.ppermute(low, "seq", outer), high, lax.ppermute(high, "seq", inner))
 
 
 def backward_body(
-    core, residual_in, branch, final_gain, reward_direction, derivative, first, second,
-    slope, out_slope_out, reward,
+    core, residual_in, b0, b1, b2, b3, final_gain, reward_direction, derivative, first, second,
+    low, high, out_slope_out, reward,
 ):
-    residual_out = residual_in[...] + sum_groups(branch)
+    residual_out = residual_in[...] + sum_halves((b0, b1, b2, b3))
     normed, inverse_std = layer_stats(residual_out)
     direction = final_gain[...] * reward_direction[...]
     reward[...] = jnp.full((8, 128), jnp.sum(normed * direction) * (1.0 / 64.0))
@@ -137,16 +150,16 @@
         back_slope = contract_rows(out_slope_out[...].astype(bf16), down[...])
         hidden_slope = (back_slope * derivative[...]).astype(bf16)
         part = matmul(hidden_slope, up[...]).astype(bf16)
-        for group in range(GROUPS):
-            slope[group] = part
+        low[...] = part[0:32]
+        high[...] = part[32:64]
 
     by_core(core, first, second, compute)
 
 
-def finish_body(group, residual_in, out_slope, slope, norm_gain, embed_weight, gradient):
+def finish_body(group, residual_in, out_slope, s0, s1, s2, s3, norm_gain, embed_weight, gradient):
     embed_rows = embed_weight[pl.ds(pl.multiple_of(group[0] * WIDTH, WIDTH), WIDTH), :]
     normed, inverse_std = layer_stats(residual_in[...])
-    weighted = sum_groups(slope) * norm_gain[...]
+    weighted = sum_halves((s0, s1, s2, s3)) * norm_gain[...]
     input_slope = out_slope[...] + layer_back(weighted, normed, inverse_std)
     pooled_slope = (0.25 * contract_rows(input_slope.astype(bf16), embed_rows)).astype(bf16)
     token = lax.broadcasted_iota(jnp.int32, (256, 64), 0)
@@ -191,11 +204,11 @@
     nearby_up = nearby[:, 0:4, :].reshape(24, EMB)
     nearby_down = nearby[:, 4:8, :].reshape(24, EMB)
     mine = jnp.where(core[0] == 0, nearby_up, nearby_down)
-    mine = lax.all_gather(mine, "x", axis=0, tiled=True)
-    first = spread_to(mine, "y", 8).reshape(HIDDEN, EMB)
+    mine = spread_to(mine, "y", 8).reshape(192, EMB)
+    first = spread_to(mine, "x", 4).reshape(HIDDEN, EMB)
     second = lax.ppermute(first, "core", [(0, 1), (1, 0)])
 
-    first, second = in_hbm(first), in_hbm(second)
+    first = in_hbm(first)
     packed = pl.pallas_call(
         pack_body, out_shape=(shape((ROWS, WIDTH), bf16),) * GROUPS, in_specs=[scalar_spec, *in_vmem(5)],
         out_specs=tuple(in_vmem(GROUPS)), name="pack",
@@ -215,26 +228,25 @@
         out_specs=pl.BlockSpec(memory_space=pltpu.VMEM), name="embed",
     )(pooled, embed_weight, position_embed)
     gain_row = norm_gain.reshape(1, EMB)
-    branch, derivative = pl.pallas_call(
-        forward_body, out_shape=(shape((GROUPS, 64, EMB), bf16), shape((64, HIDDEN), f32)),
-        in_specs=[scalar_spec, *in_vmem(4)], out_specs=tuple(in_vmem(2)),
+    half = shape((32, EMB), bf16)
+    low, high, derivative = pl.pallas_call(
+        forward_body, out_shape=(half, half, shape((64, HIDDEN), f32)),
+        in_specs=[scalar_spec, *in_vmem(4)], out_specs=tuple(in_vmem(3)),
         scratch_shapes=[pltpu.VMEM((64, EMB), bf16)], name="forward",
-    )(core, residual_in, gain_row, first, second)
-    branch = lax.all_to_all(branch, "seq", split_axis=0, concat_axis=0, tiled=True)
-    slope, out_slope, reward = pl.pallas_call(
-        backward_body,
-        out_shape=(shape((GROUPS, 64, EMB), bf16), shape((64, EMB), f32), shape((8, 128), f32)),
-        in_specs=[scalar_spec, *in_vmem(7)], out_specs=tuple(in_vmem(3)), name="backward",
+    )(core, residual_in, gain_row, first, held(second))
+    branch = group_sum(low, high)
+    low, high, out_slope, reward = pl.pallas_call(
+        backward_body, out_shape=(half, half, shape((64, EMB), f32), shape((8, 128), f32)),
+        in_specs=[scalar_spec, *in_vmem(10)], out_specs=tuple(in_vmem(4)), name="backward",
     )(
-        core, residual_in, held(branch), final_gain.reshape(1, EMB), reward_direction.reshape(1, EMB),
-        derivative, first, second,
+        core, residual_in, *map(held, branch), final_gain.reshape(1, EMB), reward_direction.reshape(1, EMB),
+        derivative, first, in_hbm(second),
     )
-    slope = lax.all_to_all(slope, "seq", split_axis=0, concat_axis=0, tiled=True)
+    slope = group_sum(low, high)
     gradient = pl.pallas_call(
-        finish_body, out_shape=shape((1, 256, WIDTH), bf16),
-        in_specs=[scalar_spec, *in_vmem(5)], out_specs=pl.BlockSpec(memory_space=pltpu.VMEM),
-        name="finish",
-    )(group, residual_in, out_slope, held(slope), gain_row, embed_weight)
+        finish_body, out_shape=shape((1, 256, WIDTH), bf16), in_specs=[scalar_spec, *in_vmem(8)],
+        out_specs=pl.BlockSpec(memory_space=pltpu.VMEM), name="finish",
+    )(group, residual_in, out_slope, *map(held, slope), gain_row, embed_weight)
     return (attended, gradient, reward[0, 0:1])
 
 

time: 250 us -> 232 us (0.928)
  the two profiles are of different devices: /device:TPU:4 before, /device:TPU:6 now
where the time goes in v3:
time: 232 us; the launch traced here: 229 us
  blocking collectives  73.6 us (32%)
  starting transfers between devices  64.6 us (28%)
  waiting for transfers between devices  52 us (22%)
  Pallas kernels  23.4 us (10%)
  local copies, waits for them, and re-layouts  9.99 us (4%)
  other arithmetic  4.48 us (2%)
    all_to_all x2, blocking collectives, spread_to(): return lax.all_to_all(copies, axes, split_axis=0, concat_axis=0, tiled=True)  53.8 us
    ppermute x3, waiting for transfers between devices, on_device(): received.append(lax.ppermute(packed[step], 'seq', around))  38.7 us
    ppermute x3, starting transfers between devices, on_device(): received.append(lax.ppermute(packed[step], 'seq', around))  21.3 us
    all_gather x1, blocking collectives, on_device(): pooled = lax.all_gather(pooled, 'seq', axis=0, tiled=False)  19.8 us
    ppermute x2, starting transfers between devices, group_sum(): lax.ppermute(low, 'seq', outer)  11.8 us
    ppermute x2, starting transfers between devices, group_sum(): high_pair = lax.ppermute(high, 'seq', outer)  10.4 us
    ppermute x2, starting transfers between devices, group_sum(): lax.ppermute(high, 'seq', inner)  7.43 us
    ppermute x2, waiting for transfers between devices, group_sum(): lax.ppermute(high, 'seq', inner)  6.59 us
  transfers between devices with their start and end apart: 13, of which 7 were waited for; matrix products, arithmetic and copies ran while one was open for 3% of the time, Pallas kernels for 4%

profile of v3, /device:TPU:6, one launch (start us, length us, event | category | flops | bytes accessed | tf_op | source)
XLA Modules:
  0.0 228.8 jit_solution(4283902665120450411)
XLA Ops:
  0.6 0.7 pad_maximum_fusion
  1.4 0.7 broadcast_in_dim.8
  2.0 5.5 %all-to-all-start = ((bf16[6,8,1408]{2,1,0:T(8,128)(2,1)}), bf16[6,8,1408]{2,1,0:T(8,128)(2,1)S(1)}, u32[]{:S(2)}, u32[]{:S(2)}) async-start(bf16[6,8,1408]{2,1,0:T(8,128)(2,1)} %broadcast_in_dim.8), calls=%async_computation | async-start | bytes 270336 | tf_op jit(solution)/shard_map/all_to_all | solution.py:194
  7.5 6.0 %all-to-all-done = bf16[6,8,1408]{2,1,0:T(8,128)(2,1)S(1)} async-done(((bf16[6,8,1408]{2,1,0:T(8,128)(2,1)}), bf16[6,8,1408]{2,1,0:T(8,128)(2,1)S(1)}, u32[]{:S(2)}, u32[]{:S(2)}) %all-to-all-start) | async-done | bytes 135200 | tf_op jit(solution)/shard_map/all_to_all | solution.py:194
  13.5 0.1 slice_select_fusion
  13.7 24.2 %all_to_all.15 = bf16[8,24,1408]{2,1,0:T(8,128)(2,1)S(1)} all-to-all(bf16[8,24,1408]{2,1,0:T(8,128)(2,1)S(1)} %broadcast_in_dim.9), channel_id=1, replica_groups=mesh['x'=4,'y'=8,'zl'=3,'core'=2,'seq'=4] {'y'}, dimensions={0} | all-to-all | bytes 1081344 | tf_op jit(solution)/shard_map/all_to_all | solution.py:194
  37.9 0.2 broadcast_in_dim.22
  38.1 29.6 %all_to_all.16 = bf16[4,192,1408]{2,1,0:T(8,128)(2,1)} all-to-all(bf16[4,192,1408]{2,1,0:T(8,128)(2,1)S(1)} %broadcast_in_dim.22), channel_id=1, replica_groups=mesh['x'=4,'y'=8,'zl'=3,'core'=2,'seq'=4] {'x'}, dimensions={0} | all-to-all | bytes 4325376 | tf_op jit(solution)/shard_map/all_to_all | solution.py:194
  67.7 1.9 collective-permute-start.3
  69.6 2.6 %pack.1 = (bf16[448,384]{1,0:T(8,128)(2,1)}, bf16[448,384]{1,0:T(8,128)(2,1)}, bf16[448,384]{1,0:T(8,128)(2,1)}, bf16[448,384]{1,0:T(8,128)(2,1)}) custom-call(s32[1]{0:T(128)} %bitcast.place.group, bf16[1,64,1536]{2,1,0:T(8,128)(2,1)} %query.1, bf16[1,64,1536]{2,1,0:T(8,128)(2,1)} %key.1, bf16[1,64,1536]{2,1,0:T(8,128)(2,1)} %value.1, ...), custom_call_target="tpu_custom_call" | custom-call | tf_op jit(solution)/shard_map/pack/pallas_call | solution.py:212
  72.1 8.2 %collective-permute-start = (bf16[448,384]{1,0:T(8,128)(2,1)}, bf16[448,384]{1,0:T(8,128)(2,1)S(1)}, u32[]{:S(2)}, u32[]{:S(2)}) collective-permute-start(bf16[448,384]{1,0:T(8,128)(2,1)} %get-tuple-element.17), channel_id=1, source_target_pairs={{0,1},{1,2},{2,3},{3,0},{4,5},{5,6},{6,7},{7,4},{8,9},{9,10},{10,1... | collective-permute-start | bytes 1032200 | tf_op jit(solution)/shard_map/ppermute | solution.py:219
  80.3 8.8 %collective-permute-start.1 = (bf16[448,384]{1,0:T(8,128)(2,1)}, bf16[448,384]{1,0:T(8,128)(2,1)S(1)}, u32[]{:S(2)}, u32[]{:S(2)}) collective-permute-start(bf16[448,384]{1,0:T(8,128)(2,1)} %get-tuple-element.18), channel_id=1, source_target_pairs={{0,2},{1,3},{2,0},{3,1},{4,6},{5,7},{6,4},{7,5},{8,10},{9,11},{10,... | collective-permute-start | bytes 1032200 | tf_op jit(solution)/shard_map/ppermute | solution.py:219
  89.2 4.3 %collective-permute-start.2 = (bf16[448,384]{1,0:T(8,128)(2,1)}, bf16[448,384]{1,0:T(8,128)(2,1)S(1)}, u32[]{:S(2)}, u32[]{:S(2)}) collective-permute-start(bf16[448,384]{1,0:T(8,128)(2,1)} %get-tuple-element.19), channel_id=1, source_target_pairs={{0,3},{1,0},{2,1},{3,2},{4,7},{5,4},{6,5},{7,6},{8,11},{9,8},{10,9... | collective-permute-start | bytes 1032200 | tf_op jit(solution)/shard_map/ppermute | solution.py:219
  93.4 0.6 reshape.49.norm_gain
  94.0 12.6 %collective-permute-done.second = bf16[448,384]{1,0:T(8,128)(2,1)S(1)} collective-permute-done((bf16[448,384]{1,0:T(8,128)(2,1)}, bf16[448,384]{1,0:T(8,128)(2,1)S(1)}, u32[]{:S(2)}, u32[]{:S(2)}) %collective-permute-start) | collective-permute-done | bytes 344096 | tf_op jit(solution)/shard_map/ppermute | solution.py:219
  106.6 0.7 copy-done.2
  107.3 20.0 %collective-permute-done.1.third = bf16[448,384]{1,0:T(8,128)(2,1)S(1)} collective-permute-done((bf16[448,384]{1,0:T(8,128)(2,1)}, bf16[448,384]{1,0:T(8,128)(2,1)S(1)}, u32[]{:S(2)}, u32[]{:S(2)}) %collective-permute-start.1) | collective-permute-done | bytes 344096 | tf_op jit(solution)/shard_map/ppermute | solution.py:219
  127.4 0.7 copy-done.4
  128.1 6.1 %collective-permute-done.2.fourth = bf16[448,384]{1,0:T(8,128)(2,1)S(1)} collective-permute-done((bf16[448,384]{1,0:T(8,128)(2,1)}, bf16[448,384]{1,0:T(8,128)(2,1)S(1)}, u32[]{:S(2)}, u32[]{:S(2)}) %collective-permute-start.2) | collective-permute-done | bytes 344096 | tf_op jit(solution)/shard_map/ppermute | solution.py:219
  134.2 0.7 copy-done.6
  135.0 1.0 copy-done.1
  135.9 1.0 copy-done.3
  136.9 1.0 copy-done.5
  137.9 1.0 copy-done.7
  138.9 2.6 %attend.1 = (bf16[1,256,384]{2,1,0:T(8,128)(2,1)}, bf16[64,384]{1,0:T(8,128)(2,1)}) custom-call(s32[1]{0:T(128)} %bitcast.place.group, bf16[448,384]{1,0:T(8,128)(2,1)S(1)} %copy-done.1, bf16[448,384]{1,0:T(8,128)(2,1)S(1)} %copy-done.3, bf16[448,384]{1,0:T(8,128)(2,1)S(1)} %copy-done.5, bf16[448,384]{1,0:T(8,128)(2,1)S(1)} %copy-done.7, f32[1,128]{1,0:T(1,128)} %bitcast.10, ...), custom_call_target="tpu_custom_call" | custom-call | tf_op jit(solution)/shard_map/attend/pallas_call | solution.py:221
  141.4 19.8 %all-gather = bf16[256,384]{1,0:T(8,128)(2,1)} all-gather(bf16[64,384]{1,0:T(8,128)(2,1)} %get-tuple-element.21), channel_id=2, replica_groups=mesh['x'=4,'y'=8,'zl'=3,'core'=2,'seq'=4] {'seq'}, dimensions={0}, use_global_device_ids=true | all-gather | bytes 245760 | tf_op jit(solution)/shard_map/all_gather | solution.py:225
  161.2 3.9 %embed.1.residual_in = f32[64,1408]{1,0:T(8,128)} custom-call(bf16[4,64,384]{2,1,0:T(8,128)(2,1)} %bitcast.9, bf16[1536,1408]{1,0:T(8,128)(2,1)} %embed_weight.3, f32[64,1408]{1,0:T(8,128)} %position_embed.1), custom_call_target="tpu_custom_call" | custom-call | tf_op jit(solution)/shard_map/embed/pallas_call | solution.py:226
  165.1 5.0 %forward.1 = (bf16[32,1408]{1,0:T(8,128)(2,1)}, bf16[32,1408]{1,0:T(8,128)(2,1)}, f32[64,768]{1,0:T(8,128)}) custom-call(s32[1]{0:T(128)} %bitcast.4.core, f32[64,1408]{1,0:T(8,128)} %embed.1.residual_in, f32[1,1408]{1,0:T(1,128)} %reshape.49.norm_gain, bf16[768,1408]{1,0:T(8,128)(2,1)} %bitcast.6.first, bf16[768,1408]{1,0:T(8,128)(2,1)S(1)} %collective-permute-done.3.second), custom_call_target="tpu_custom_call" | custom-call | tf_op jit(solution)/shard_map/forward/pallas_call | solution.py:232
  170.1 3.8 %collective-permute-start.4 = (bf16[32,1408]{1,0:T(8,128)(2,1)}, bf16[32,1408]{1,0:T(8,128)(2,1)S(1)}, u32[]{:S(2)}, u32[]{:S(2)}) collective-permute-start(bf16[32,1408]{1,0:T(8,128)(2,1)} %get-tuple-element.22), channel_id=1, source_target_pairs={{0,1},{1,0},{2,3},{3,2},{4,5},{5,4},{6,7},{7,6},{8,9},{9,8},{10,11... | collective-permute-start | bytes 270344 | tf_op jit(solution)/shard_map/ppermute | solution.py:133
  174.0 5.0 %collective-permute-start.6 = (bf16[32,1408]{1,0:T(8,128)(2,1)}, bf16[32,1408]{1,0:T(8,128)(2,1)S(1)}, u32[]{:S(2)}, u32[]{:S(2)}) collective-permute-start(bf16[32,1408]{1,0:T(8,128)(2,1)} %get-tuple-element.23), channel_id=1, source_target_pairs={{0,3},{3,0},{1,2},{2,1},{4,7},{7,4},{5,6},{6,5},{8,11},{11,8},{9,1... | collective-permute-start | bytes 270344 | tf_op jit(solution)/shard_map/ppermute | solution.py:134
  179.0 0.9 add_convert_fusion.3.b0
  179.9 6.9 %collective-permute-start.5 = (bf16[32,1408]{1,0:T(8,128)(2,1)S(1)}, bf16[32,1408]{1,0:T(8,128)(2,1)S(1)}, u32[]{:S(2)}, u32[]{:S(2)}) collective-permute-start(bf16[32,1408]{1,0:T(8,128)(2,1)S(1)} %add_convert_fusion.3.b0), channel_id=1, source_target_pairs={{0,3},{3,0},{1,2},{2,1},{4,7},{7,4},{5,6},{6,5},{8,11},{11,8},{9,1... | collective-permute-start | bytes 270344 | tf_op jit(solution)/shard_map/ppermute | solution.py:136
  186.8 0.9 add_convert_fusion.2.b2
  187.7 2.5 %collective-permute-start.7 = (bf16[32,1408]{1,0:T(8,128)(2,1)S(1)}, bf16[32,1408]{1,0:T(8,128)(2,1)S(1)}, u32[]{:S(2)}, u32[]{:S(2)}) collective-permute-start(bf16[32,1408]{1,0:T(8,128)(2,1)S(1)} %add_convert_fusion.2.b2), channel_id=1, source_target_pairs={{0,1},{1,0},{2,3},{3,2},{4,5},{5,4},{6,7},{7,6},{8,9},{9,8},{10,11... | collective-permute-start | bytes 270344 | tf_op jit(solution)/shard_map/ppermute | solution.py:136
  190.3 0.6 reshape.51.final_gain
  190.9 0.6 reshape.52.reward_direction
  191.5 4.5 %collective-permute-done.7.b3 = bf16[32,1408]{1,0:T(8,128)(2,1)S(1)} collective-permute-done((bf16[32,1408]{1,0:T(8,128)(2,1)S(1)}, bf16[32,1408]{1,0:T(8,128)(2,1)S(1)}, u32[]{:S(2)}, u32[]{:S(2)}) %collective-permute-start.7) | collective-permute-done | bytes 90144 | tf_op jit(solution)/shard_map/ppermute | solution.py:136
  196.0 5.2 %backward.1 = (bf16[32,1408]{1,0:T(8,128)(2,1)}, bf16[32,1408]{1,0:T(8,128)(2,1)}, f32[64,1408]{1,0:T(8,128)}, f32[8,128]{1,0:T(8,128)}) custom-call(s32[1]{0:T(128)} %bitcast.4.core, f32[64,1408]{1,0:T(8,128)} %embed.1.residual_in, bf16[32,1408]{1,0:T(8,128)(2,1)S(1)} %add_convert_fusion.3.b0, bf16[32,1408]{1,0:T(8,128)(2,1)S(1)} %collective-permute-done.5.b1, ...), custom_call_target="tpu_custom_call" | custom-call | tf_op jit(solution)/shard_map/backward/pallas_call | solution.py:238
  201.2 2.5 %collective-permute-start.8 = (bf16[32,1408]{1,0:T(8,128)(2,1)}, bf16[32,1408]{1,0:T(8,128)(2,1)S(1)}, u32[]{:S(2)}, u32[]{:S(2)}) collective-permute-start(bf16[32,1408]{1,0:T(8,128)(2,1)} %get-tuple-element.26), channel_id=1, source_target_pairs={{0,1},{1,0},{2,3},{3,2},{4,5},{5,4},{6,7},{7,6},{8,9},{9,8},{10,11... | collective-permute-start | bytes 270344 | tf_op jit(solution)/shard_map/ppermute | solution.py:133
  203.7 5.4 %collective-permute-start.10 = (bf16[32,1408]{1,0:T(8,128)(2,1)}, bf16[32,1408]{1,0:T(8,128)(2,1)S(1)}, u32[]{:S(2)}, u32[]{:S(2)}) collective-permute-start(bf16[32,1408]{1,0:T(8,128)(2,1)} %get-tuple-element.27), channel_id=1, source_target_pairs={{0,3},{3,0},{1,2},{2,1},{4,7},{7,4},{5,6},{6,5},{8,11},{11,8},{9,1... | collective-permute-start | bytes 270344 | tf_op jit(solution)/shard_map/ppermute | solution.py:134
  209.1 0.6 collective-permute-done.8
  209.7 0.9 add_convert_fusion.1.s0
  210.6 4.9 %collective-permute-start.9 = (bf16[32,1408]{1,0:T(8,128)(2,1)S(1)}, bf16[32,1408]{1,0:T(8,128)(2,1)S(1)}, u32[]{:S(2)}, u32[]{:S(2)}) collective-permute-start(bf16[32,1408]{1,0:T(8,128)(2,1)S(1)} %add_convert_fusion.1.s0), channel_id=1, source_target_pairs={{0,3},{3,0},{1,2},{2,1},{4,7},{7,4},{5,6},{6,5},{8,11},{11,8},{9,1... | collective-permute-start | bytes 270344 | tf_op jit(solution)/shard_map/ppermute | solution.py:136
  215.5 0.9 add_convert_fusion.s2
  216.5 4.9 %collective-permute-start.11 = (bf16[32,1408]{1,0:T(8,128)(2,1)S(1)}, bf16[32,1408]{1,0:T(8,128)(2,1)S(1)}, u32[]{:S(2)}, u32[]{:S(2)}) collective-permute-start(bf16[32,1408]{1,0:T(8,128)(2,1)S(1)} %add_convert_fusion.s2), channel_id=1, source_target_pairs={{0,1},{1,0},{2,3},{3,2},{4,5},{5,4},{6,7},{7,6},{8,9},{9,8},{10,11... | collective-permute-start | bytes 270344 | tf_op jit(solution)/shard_map/ppermute | solution.py:136
  221.4 1.2 slice.11
  222.6 2.1 collective-permute-done.11.s3
  224.7 4.2 %finish.1 = bf16[1,256,384]{2,1,0:T(8,128)(2,1)} custom-call(s32[1]{0:T(128)} %bitcast.place.group, f32[64,1408]{1,0:T(8,128)} %embed.1.residual_in, f32[64,1408]{1,0:T(8,128)} %get-tuple-element.25.out_slope, bf16[32,1408]{1,0:T(8,128)(2,1)S(1)} %add_convert_fusion.1.s0, bf16[32,1408]{1,0:T(8,128)(2,1)S(1)} %collective-permute-done.9.s1, ...), custom_call_target="tpu_custom_call" | custom-call | tf_op jit(solution)/shard_map/finish/pallas_call | solution.py:246
  (23 shorter events, 0.1 us)
Async XLA Ops:
  2.0 11.5 %all-to-all-start = ((bf16[6,8,1408]{2,1,0:T(8,128)(2,1)}), bf16[6,8,1408]{2,1,0:T(8,128)(2,1)S(1)}, u32[]{:S(2)}, u32[]{:S(2)}) async-start(bf16[6,8,1408]{2,1,0:T(8,128)(2,1)} %broadcast_in_dim.8), calls=%async_computation | async-start | bytes 270336 | tf_op jit(solution)/shard_map/all_to_all | solution.py:194
  38.1 55.4 %copy-start.8 = (f32[1408]{0:T(1024)S(1)}, f32[1408]{0:T(1024)}, u32[]{:S(2)}) copy-start(f32[1408]{0:T(1024)} %param.23) | copy-start | bytes 16900
  67.7 97.5 %collective-permute-start.3 = (bf16[768,1408]{1,0:T(8,128)(2,1)}, bf16[768,1408]{1,0:T(8,128)(2,1)S(1)}, u32[]{:S(2)}, u32[]{:S(2)}) collective-permute-start(bf16[768,1408]{1,0:T(8,128)(2,1)} %bitcast.6.first), channel_id=1, source_target_pairs={{0,4},{4,0},{1,5},{5,1},{2,6},{6,2},{3,7},{7,3},{8,12},{12,8},{9,1... | collective-permute-start | bytes 6488072 | tf_op jit(solution)/shard_map/ppermute | solution.py:209
  72.1 34.5 %collective-permute-start = (bf16[448,384]{1,0:T(8,128)(2,1)}, bf16[448,384]{1,0:T(8,128)(2,1)S(1)}, u32[]{:S(2)}, u32[]{:S(2)}) collective-permute-start(bf16[448,384]{1,0:T(8,128)(2,1)} %get-tuple-element.17), channel_id=1, source_target_pairs={{0,1},{1,2},{2,3},{3,0},{4,5},{5,6},{6,7},{7,4},{8,9},{9,10},{10,1... | collective-permute-start | bytes 1032200 | tf_op jit(solution)/shard_map/ppermute | solution.py:219
  80.3 47.0 %collective-permute-start.1 = (bf16[448,384]{1,0:T(8,128)(2,1)}, bf16[448,384]{1,0:T(8,128)(2,1)S(1)}, u32[]{:S(2)}, u32[]{:S(2)}) collective-permute-start(bf16[448,384]{1,0:T(8,128)(2,1)} %get-tuple-element.18), channel_id=1, source_target_pairs={{0,2},{1,3},{2,0},{3,1},{4,6},{5,7},{6,4},{7,5},{8,10},{9,11},{10,... | collective-permute-start | bytes 1032200 | tf_op jit(solution)/shard_map/ppermute | solution.py:219
  89.2 45.1 %collective-permute-start.2 = (bf16[448,384]{1,0:T(8,128)(2,1)}, bf16[448,384]{1,0:T(8,128)(2,1)S(1)}, u32[]{:S(2)}, u32[]{:S(2)}) collective-permute-start(bf16[448,384]{1,0:T(8,128)(2,1)} %get-tuple-element.19), channel_id=1, source_target_pairs={{0,3},{1,0},{2,1},{3,2},{4,7},{5,4},{6,5},{7,6},{8,11},{9,8},{10,9... | collective-permute-start | bytes 1032200 | tf_op jit(solution)/shard_map/ppermute | solution.py:219
  106.6 0.7 copy-start.2
  127.4 0.7 copy-start.4
  134.2 0.7 copy-start.6
  135.0 1.0 copy-start.1
  135.9 1.0 copy-start.3
  136.9 1.0 copy-start.5
  137.9 1.0 copy-start.7
  165.1 5.0 %copy-start = (bf16[768,1408]{1,0:T(8,128)(2,1)}, bf16[768,1408]{1,0:T(8,128)(2,1)S(1)}, u32[]{:S(2)}) copy-start(bf16[768,1408]{1,0:T(8,128)(2,1)S(1)} %collective-permute-done.3.second) | copy-start | bytes 6488068
  165.1 25.2 %copy-start.9 = (f32[1408]{0:T(1024)S(1)}, f32[1408]{0:T(1024)}, u32[]{:S(2)}) copy-start(f32[1408]{0:T(1024)} %param.24) | copy-start | bytes 16900
  165.1 25.8 %copy-start.10 = (f32[1408]{0:T(1024)S(1)}, f32[1408]{0:T(1024)}, u32[]{:S(2)}) copy-start(f32[1408]{0:T(1024)} %param.27) | copy-start | bytes 16900
  170.1 8.9 %collective-permute-start.4 = (bf16[32,1408]{1,0:T(8,128)(2,1)}, bf16[32,1408]{1,0:T(8,128)(2,1)S(1)}, u32[]{:S(2)}, u32[]{:S(2)}) collective-permute-start(bf16[32,1408]{1,0:T(8,128)(2,1)} %get-tuple-element.22), channel_id=1, source_target_pairs={{0,1},{1,0},{2,3},{3,2},{4,5},{5,4},{6,7},{7,6},{8,9},{9,8},{10,11... | collective-permute-start | bytes 270344 | tf_op jit(solution)/shard_map/ppermute | solution.py:133
  174.0 12.9 %collective-permute-start.6 = (bf16[32,1408]{1,0:T(8,128)(2,1)}, bf16[32,1408]{1,0:T(8,128)(2,1)S(1)}, u32[]{:S(2)}, u32[]{:S(2)}) collective-permute-start(bf16[32,1408]{1,0:T(8,128)(2,1)} %get-tuple-element.23), channel_id=1, source_target_pairs={{0,3},{3,0},{1,2},{2,1},{4,7},{7,4},{5,6},{6,5},{8,11},{11,8},{9,1... | collective-permute-start | bytes 270344 | tf_op jit(solution)/shard_map/ppermute | solution.py:134
  179.9 11.6 %collective-permute-start.5 = (bf16[32,1408]{1,0:T(8,128)(2,1)S(1)}, bf16[32,1408]{1,0:T(8,128)(2,1)S(1)}, u32[]{:S(2)}, u32[]{:S(2)}) collective-permute-start(bf16[32,1408]{1,0:T(8,128)(2,1)S(1)} %add_convert_fusion.3.b0), channel_id=1, source_target_pairs={{0,3},{3,0},{1,2},{2,1},{4,7},{7,4},{5,6},{6,5},{8,11},{11,8},{9,1... | collective-permute-start | bytes 270344 | tf_op jit(solution)/shard_map/ppermute | solution.py:136
  187.7 8.2 %collective-permute-start.7 = (bf16[32,1408]{1,0:T(8,128)(2,1)S(1)}, bf16[32,1408]{1,0:T(8,128)(2,1)S(1)}, u32[]{:S(2)}, u32[]{:S(2)}) collective-permute-start(bf16[32,1408]{1,0:T(8,128)(2,1)S(1)} %add_convert_fusion.2.b2), channel_id=1, source_target_pairs={{0,1},{1,0},{2,3},{3,2},{4,5},{5,4},{6,7},{7,6},{8,9},{9,8},{10,11... | collective-permute-start | bytes 270344 | tf_op jit(solution)/shard_map/ppermute | solution.py:136
  201.2 8.5 %collective-permute-start.8 = (bf16[32,1408]{1,0:T(8,128)(2,1)}, bf16[32,1408]{1,0:T(8,128)(2,1)S(1)}, u32[]{:S(2)}, u32[]{:S(2)}) collective-permute-start(bf16[32,1408]{1,0:T(8,128)(2,1)} %get-tuple-element.26), channel_id=1, source_target_pairs={{0,1},{1,0},{2,3},{3,2},{4,5},{5,4},{6,7},{7,6},{8,9},{9,8},{10,11... | collective-permute-start | bytes 270344 | tf_op jit(solution)/shard_map/ppermute | solution.py:133
  203.7 11.8 %collective-permute-start.10 = (bf16[32,1408]{1,0:T(8,128)(2,1)}, bf16[32,1408]{1,0:T(8,128)(2,1)S(1)}, u32[]{:S(2)}, u32[]{:S(2)}) collective-permute-start(bf16[32,1408]{1,0:T(8,128)(2,1)} %get-tuple-element.27), channel_id=1, source_target_pairs={{0,3},{3,0},{1,2},{2,1},{4,7},{7,4},{5,6},{6,5},{8,11},{11,8},{9,1... | collective-permute-start | bytes 270344 | tf_op jit(solution)/shard_map/ppermute | solution.py:134
  210.6 11.9 %collective-permute-start.9 = (bf16[32,1408]{1,0:T(8,128)(2,1)S(1)}, bf16[32,1408]{1,0:T(8,128)(2,1)S(1)}, u32[]{:S(2)}, u32[]{:S(2)}) collective-permute-start(bf16[32,1408]{1,0:T(8,128)(2,1)S(1)} %add_convert_fusion.1.s0), channel_id=1, source_target_pairs={{0,3},{3,0},{1,2},{2,1},{4,7},{7,4},{5,6},{6,5},{8,11},{11,8},{9,1... | collective-permute-start | bytes 270344 | tf_op jit(solution)/shard_map/ppermute | solution.py:136
  216.5 8.2 %collective-permute-start.11 = (bf16[32,1408]{1,0:T(8,128)(2,1)S(1)}, bf16[32,1408]{1,0:T(8,128)(2,1)S(1)}, u32[]{:S(2)}, u32[]{:S(2)}) collective-permute-start(bf16[32,1408]{1,0:T(8,128)(2,1)S(1)} %add_convert_fusion.s2), channel_id=1, source_target_pairs={{0,1},{1,0},{2,3},{3,2},{4,5},{5,4},{6,7},{7,6},{8,9},{9,8},{10,11... | collective-permute-start | bytes 270344 | tf_op jit(solution)/shard_map/ppermute | solution.py:136

commit v4 on v3

--- a/solution.py
+++ b/solution.py
@@ -21,7 +21,16 @@
 bf16 = jnp.bfloat16
 
 
-def pack_body(place, query, key, value, text_key, text_value, *packed):
+def pack_body(
+    place, query, key, value, text_key, text_value, norm_gain, final_gain, reward_direction, up, down,
+    p0, p1, p2, p3, gain_row, direction_row, copies,
+):
+    rows = jnp.concatenate([up[...], down[...]], axis=0)
+    for member in range(6):
+        copies[member] = rows
+    gain_row[...] = norm_gain[...].reshape(1, EMB)
+    direction_row[...] = (final_gain[...] * reward_direction[...]).reshape(1, EMB)
+    packed = (p0, p1, p2, p3)
     for step in range(GROUPS):
         group = (place[0] + step) % GROUPS
         cols = pl.ds(pl.multiple_of(group * WIDTH, HEAD), WIDTH)
@@ -84,10 +93,17 @@
     )
 
 
-def embed_body(pooled, embed_weight, position_embed, residual_in):
+def embed_body(pooled, embed_weight, position_embed, residual_in, weight, sems):
+    def part(group):
+        rows = pl.ds(group * WIDTH, WIDTH)
+        return pltpu.make_async_copy(embed_weight.at[rows, :], weight.at[rows, :], sems.at[group])
+
+    for group in range(GROUPS):
+        part(group).start()
     total = position_embed[...]
     for group in range(GROUPS):
-        total = total + matmul(pooled[group], embed_weight[group * WIDTH : (group + 1) * WIDTH, :])
+        part(group).wait()
+        total = total + matmul(pooled[group], weight[group * WIDTH : (group + 1) * WIDTH, :])
     residual_in[...] = total
 
 
@@ -101,9 +117,12 @@
         compute(second, first)
 
 
-def forward_body(core, residual_in, norm_gain, first, second, low, high, derivative_out, hidden):
+def forward_body(core, residual_in, norm_gain, first_rows, second, low, high, derivative_out, hidden, first, sem):
+    fetch = pltpu.make_async_copy(first_rows, first, sem)
+    fetch.start()
     normed, _ = layer_stats(residual_in[...])
     hidden[...] = (normed * norm_gain[...]).astype(bf16)
+    fetch.wait()
 
     def compute(up, down):
         preact = contract_rows(hidden[...], up[...])
@@ -137,37 +156,49 @@
 
 
 def backward_body(
-    core, residual_in, b0, b1, b2, b3, final_gain, reward_direction, derivative, first, second,
-    low, high, out_slope_out, reward,
+    core, residual_in, b0, b1, b2, b3, norm_gain, direction_row, derivative, first_rows, second_rows, embed_rows,
+    blocks, reward, out_slope, part, first, second, embed_weight, sems,
 ):
+    copies = [
+        pltpu.make_async_copy(first_rows, first, sems.at[0]),
+        pltpu.make_async_copy(second_rows, second, sems.at[1]),
+        pltpu.make_async_copy(embed_rows, embed_weight, sems.at[2]),
+    ]
+    for copy in copies:
+        copy.start()
     residual_out = residual_in[...] + sum_halves((b0, b1, b2, b3))
     normed, inverse_std = layer_stats(residual_out)
-    direction = final_gain[...] * reward_direction[...]
-    reward[...] = jnp.full((8, 128), jnp.sum(normed * direction) * (1.0 / 64.0))
-    out_slope_out[...] = layer_back(direction, normed, inverse_std)
+    direction = direction_row[...]
+    reward[0] = jnp.sum(normed * direction) * (1.0 / 64.0)
+    out_slope[...] = layer_back(direction, normed, inverse_std)
+    copies[0].wait()
+    copies[1].wait()
 
     def compute(up, down):
-        back_slope = contract_rows(out_slope_out[...].astype(bf16), down[...])
+        back_slope = contract_rows(out_slope[...].astype(bf16), down[...])
         hidden_slope = (back_slope * derivative[...]).astype(bf16)
-        part = matmul(hidden_slope, up[...]).astype(bf16)
-        low[...] = part[0:32]
-        high[...] = part[32:64]
+        part[...] = matmul(hidden_slope, up[...])
 
     by_core(core, first, second, compute)
-
-
-def finish_body(group, residual_in, out_slope, s0, s1, s2, s3, norm_gain, embed_weight, gradient):
-    embed_rows = embed_weight[pl.ds(pl.multiple_of(group[0] * WIDTH, WIDTH), WIDTH), :]
     normed, inverse_std = layer_stats(residual_in[...])
-    weighted = sum_halves((s0, s1, s2, s3)) * norm_gain[...]
-    input_slope = out_slope[...] + layer_back(weighted, normed, inverse_std)
-    pooled_slope = (0.25 * contract_rows(input_slope.astype(bf16), embed_rows)).astype(bf16)
+    share = layer_back(part[...] * norm_gain[...], normed, inverse_std)
+    share = (share + 0.25 * out_slope[...]).astype(bf16)
+    copies[2].wait()
+    for group in range(GROUPS):
+        rows = slice(group * WIDTH, (group + 1) * WIDTH)
+        blocks[group] = (0.25 * contract_rows(share, embed_weight[rows, :])).astype(bf16)
+
+
+def finish_body(blocks, gradient):
+    pooled_slope = blocks[0].astype(f32)
+    for group in range(1, GROUPS):
+        pooled_slope = pooled_slope + blocks[group].astype(f32)
     token = lax.broadcasted_iota(jnp.int32, (256, 64), 0)
     reward_token = lax.broadcasted_iota(jnp.int32, (256, 64), 1)
     same_row = (token >> 6) == (reward_token >> 4)
     same_col = ((token & 31) >> 1) == (reward_token & 15)
     spread = jnp.where(same_row & same_col, 1.0, 0.0).astype(bf16)
-    gradient[0] = matmul(spread, pooled_slope).astype(bf16)
+    gradient[0] = matmul(spread, pooled_slope.astype(bf16)).astype(bf16)
 
 
 def shape(dims, dtype):
@@ -176,6 +207,10 @@
 
 def held(value):
     return pltpu.with_memory_space_constraint(value, pltpu.VMEM)
+
+
+def in_any(count):
+    return [pl.BlockSpec(memory_space=pl.ANY)] * count
 
 
 def in_hbm(value):
@@ -200,7 +235,19 @@
 ):
     core = lax.axis_index("core").astype(jnp.int32).reshape(1)
     group = lax.axis_index("seq").astype(jnp.int32).reshape(1)
-    nearby = spread_to(jnp.concatenate([up_weight, down_weight], axis=0), ("zl", "core"), 6)
+    packed = pl.pallas_call(
+        pack_body,
+        out_shape=(
+            *(shape((ROWS, WIDTH), bf16),) * GROUPS, shape((1, EMB), f32), shape((1, EMB), f32),
+            shape((6, 8, EMB), bf16),
+        ),
+        in_specs=[scalar_spec, *in_vmem(10)], out_specs=tuple(in_vmem(7)), name="pack",
+    )(
+        group, image_query, image_key, image_value, text_key, text_value, norm_gain, final_gain,
+        reward_direction, up_weight, down_weight,
+    )
+    *packed, gain_row, direction_row, copies = packed
+    nearby = lax.all_to_all(copies, ("zl", "core"), split_axis=0, concat_axis=0, tiled=True)
     nearby_up = nearby[:, 0:4, :].reshape(24, EMB)
     nearby_down = nearby[:, 4:8, :].reshape(24, EMB)
     mine = jnp.where(core[0] == 0, nearby_up, nearby_down)
@@ -209,10 +256,6 @@
     second = lax.ppermute(first, "core", [(0, 1), (1, 0)])
 
     first = in_hbm(first)
-    packed = pl.pallas_call(
-        pack_body, out_shape=(shape((ROWS, WIDTH), bf16),) * GROUPS, in_specs=[scalar_spec, *in_vmem(5)],
-        out_specs=tuple(in_vmem(GROUPS)), name="pack",
-    )(group, image_query, image_key, image_value, text_key, text_value)
     received = [packed[0]]
     for step in (2, 1, 3):
         around = [(member, (member + step) % GROUPS) for member in range(GROUPS)]
@@ -224,30 +267,38 @@
     )(group, *map(held, received), query_gain.reshape(1, HEAD), key_gain.reshape(1, HEAD))
     pooled = lax.all_gather(pooled, "seq", axis=0, tiled=False)
     residual_in = pl.pallas_call(
-        embed_body, out_shape=shape((64, EMB), f32), in_specs=in_vmem(3),
-        out_specs=pl.BlockSpec(memory_space=pltpu.VMEM), name="embed",
+        embed_body, out_shape=shape((64, EMB), f32),
+        in_specs=[in_vmem(1)[0], *in_any(1), *in_vmem(1)], out_specs=pl.BlockSpec(memory_space=pltpu.VMEM),
+        scratch_shapes=[pltpu.VMEM((1536, EMB), bf16), pltpu.SemaphoreType.DMA((GROUPS,))], name="embed",
     )(pooled, embed_weight, position_embed)
-    gain_row = norm_gain.reshape(1, EMB)
     half = shape((32, EMB), bf16)
     low, high, derivative = pl.pallas_call(
         forward_body, out_shape=(half, half, shape((64, HIDDEN), f32)),
-        in_specs=[scalar_spec, *in_vmem(4)], out_specs=tuple(in_vmem(3)),
-        scratch_shapes=[pltpu.VMEM((64, EMB), bf16)], name="forward",
+        in_specs=[scalar_spec, *in_vmem(2), *in_any(1), *in_vmem(1)], out_specs=tuple(in_vmem(3)),
+        scratch_shapes=[
+            pltpu.VMEM((64, EMB), bf16), pltpu.VMEM((HIDDEN, EMB), bf16), pltpu.SemaphoreType.DMA,
+        ],
+        name="forward",
     )(core, residual_in, gain_row, first, held(second))
     branch = group_sum(low, high)
-    low, high, out_slope, reward = pl.pallas_call(
-        backward_body, out_shape=(half, half, shape((64, EMB), f32), shape((8, 128), f32)),
-        in_specs=[scalar_spec, *in_vmem(10)], out_specs=tuple(in_vmem(4)), name="backward",
+    blocks, reward = pl.pallas_call(
+        backward_body, out_shape=(shape((GROUPS, 64, WIDTH), bf16), shape((1,), f32)),
+        in_specs=[scalar_spec, *in_vmem(8), *in_any(3)], out_specs=(in_vmem(1)[0], scalar_spec),
+        scratch_shapes=[
+            pltpu.VMEM((64, EMB), f32), pltpu.VMEM((64, EMB), f32), pltpu.VMEM((HIDDEN, EMB), bf16),
+            pltpu.VMEM((HIDDEN, EMB), bf16), pltpu.VMEM((1536, EMB), bf16), pltpu.SemaphoreType.DMA((3,)),
+        ],
+        name="backward",
     )(
-        core, residual_in, *map(held, branch), final_gain.reshape(1, EMB), reward_direction.reshape(1, EMB),
-        derivative, first, in_hbm(second),
+        core, residual_in, *map(held, branch), gain_row, direction_row, derivative, first, in_hbm(second),
+        embed_weight,
     )
-    slope = group_sum(low, high)
+    blocks = lax.all_to_all(blocks, "seq", split_axis=0, concat_axis=0, tiled=True)
     gradient = pl.pallas_call(
-        finish_body, out_shape=shape((1, 256, WIDTH), bf16), in_specs=[scalar_spec, *in_vmem(8)],
+        finish_body, out_shape=shape((1, 256, WIDTH), bf16), in_specs=in_vmem(1),
         out_specs=pl.BlockSpec(memory_space=pltpu.VMEM), name="finish",
-    )(group, residual_in, out_slope, *map(held, slope), gain_row, embed_weight)
-    return (attended, gradient, reward[0, 0:1])
+    )(held(blocks))
+    return (attended, gradient, reward)
 
 
 def solution(mesh):

time: 232 us -> 219 us (0.944)
  blocking collectives: 73.6 us -> 91.8 us
  starting transfers between devices: 64.6 us -> 46.8 us
  local copies, waits for them, and re-layouts: 9.99 us -> 0.24 us
  other arithmetic: 4.48 us -> 1.9 us
    all_to_all x0 -> x1, blocking collectives: none -> 18.1 us  [on_device(): lax.all_to_all(blocks, 'seq', split_axis=0, concat_axis=0, tiled=True)]
    unnamed x22 -> x10, local copies, waits for them, and re-layouts: 6.12 us -> 0.02 us
    ppermute x2 -> x1, starting transfers between devices: 10.4 us -> 4.72 us  [group_sum(): high_pair = lax.ppermute(high, 'seq', outer)]
    ppermute x2 -> x1, starting transfers between devices: 7.43 us -> 1.92 us  [group_sum(): lax.ppermute(high, 'seq', inner)]
    ppermute x2 -> x1, starting transfers between devices: 11.8 us -> 7.38 us  [group_sum(): lax.ppermute(low, 'seq', outer)]
    pallas_call x1, Pallas kernels: 4.15 us -> 0.88 us  [on_device(): pl.pallas_call(finish_body, out_shape=shape((1, 256, WIDTH), bf16), in_sp...]
    pallas_call x3, Pallas kernels: 11.7 us -> 14.4 us  [the longest x1 7.38 us: on_device(): pl.pallas_call(backward_body, out_shape=(shape((GROUPS, 64, WIDTH), bf16)...]
    ppermute x2 -> x1, starting transfers between devices: 6.35 us -> 4.14 us  [group_sum(): low_pair = lax.ppermute(low, 'seq', inner)]
  transfers between devices with their start and end apart: 13 -> 9, of which waited for: 7 -> 6; matrix products, arithmetic and copies ran while one was open for 3% -> 1% of each run, Pallas kernels for 4% -> 3%
where the time goes in v4:
time: 219 us; the launch traced here: 217 us
  blocking collectives  91.8 us (42%)
  waiting for transfers between devices  52.9 us (24%)
  starting transfers between devices  46.8 us (21%)
  Pallas kernels  23 us (11%)
    all_to_all x2, blocking collectives, spread_to(): return lax.all_to_all(copies, axes, split_axis=0, concat_axis=0, tiled=True)  53.9 us
    ppermute x3, waiting for transfers between devices, on_device(): received.append(lax.ppermute(packed[step], 'seq', around))  40.6 us
    ppermute x3, starting transfers between devices, on_device(): received.append(lax.ppermute(packed[step], 'seq', around))  21.3 us
    all_gather x1, blocking collectives, on_device(): pooled = lax.all_gather(pooled, 'seq', axis=0, tiled=False)  19.7 us
    all_to_all x1, blocking collectives, on_device(): lax.all_to_all(blocks, 'seq', split_axis=0, concat_axis=0, tiled=True)  18.1 us
    pallas_call x1, Pallas kernels, on_device(): pl.pallas_call(backward_body, out_shape=(shape((GROUPS, 64, WIDTH), bf16)...  7.38 us
    ppermute x1, starting transfers between devices, group_sum(): lax.ppermute(low, 'seq', outer)  7.38 us
    all_to_all x1, waiting for transfers between devices, on_device(): lax.all_to_all(copies, ('zl', 'core'), split_axis=0, concat_axis=0, tiled...  6.03 us
  transfers between devices with their start and end apart: 9, of which 6 were waited for; matrix products, arithmetic and copies ran while one was open for 1% of the time, Pallas kernels for 3%

profile of v4, /device:TPU:6, one launch (start us, length us, event | category | flops | bytes accessed | tf_op | source)
XLA Modules:
  0.0 217.4 jit_solution(11586236380820171712)
XLA Ops:
  0.6 2.6 %pack.1 = (bf16[448,384]{1,0:T(8,128)(2,1)}, bf16[448,384]{1,0:T(8,128)(2,1)}, bf16[448,384]{1,0:T(8,128)(2,1)}, bf16[448,384]{1,0:T(8,128)(2,1)}, f32[1,1408]{1...) custom-call(s32[1]{0:T(128)} %bitcast.place, bf16[1,64,1536]{2,1,0:T(8,128)(2,1)} %query.1, ...), custom_call_target="tpu_custom_call" | custom-call | tf_op jit(solution)/shard_map/pack/pallas_call | solution.py:238
  3.3 5.5 %all-to-all-start = ((bf16[6,8,1408]{2,1,0:T(8,128)(2,1)}), bf16[6,8,1408]{2,1,0:T(8,128)(2,1)S(1)}, u32[]{:S(2)}, u32[]{:S(2)}) async-start(bf16[6,8,1408]{2,1,0:T(8,128)(2,1)} %get-tuple-element.24), calls=%async_computation | async-start | bytes 270336 | tf_op jit(solution)/shard_map/all_to_all | solution.py:250
  8.7 6.0 %all-to-all-done = bf16[6,8,1408]{2,1,0:T(8,128)(2,1)S(1)} async-done(((bf16[6,8,1408]{2,1,0:T(8,128)(2,1)}), bf16[6,8,1408]{2,1,0:T(8,128)(2,1)S(1)}, u32[]{:S(2)}, u32[]{:S(2)}) %all-to-all-start) | async-done | bytes 135200 | tf_op jit(solution)/shard_map/all_to_all | solution.py:250
  14.8 0.1 slice_select_fusion
  14.9 24.2 %all_to_all.20 = bf16[8,24,1408]{2,1,0:T(8,128)(2,1)S(1)} all-to-all(bf16[8,24,1408]{2,1,0:T(8,128)(2,1)S(1)} %broadcast_in_dim.6), channel_id=1, replica_groups=mesh['x'=4,'y'=8,'zl'=3,'core'=2,'seq'=4] {'y'}, dimensions={0} | all-to-all | bytes 1081344 | tf_op jit(solution)/shard_map/all_to_all | solution.py:229
  39.1 0.2 broadcast_in_dim.15
  39.3 0.0 copy-start.4
  39.3 0.0 copy-start.3
  39.3 0.0 copy-start.2
  39.3 0.0 copy-start.1
  39.3 29.7 %all_to_all.21 = bf16[4,192,1408]{2,1,0:T(8,128)(2,1)} all-to-all(bf16[4,192,1408]{2,1,0:T(8,128)(2,1)S(1)} %broadcast_in_dim.15), channel_id=1, replica_groups=mesh['x'=4,'y'=8,'zl'=3,'core'=2,'seq'=4] {'x'}, dimensions={0} | all-to-all | bytes 4325376 | tf_op jit(solution)/shard_map/all_to_all | solution.py:229
  69.0 1.9 collective-permute-start.3
  71.0 0.0 copy-done.4
  71.0 8.2 %collective-permute-start = (bf16[448,384]{1,0:T(8,128)(2,1)S(1)}, bf16[448,384]{1,0:T(8,128)(2,1)S(1)}, u32[]{:S(2)}, u32[]{:S(2)}) collective-permute-start(bf16[448,384]{1,0:T(8,128)(2,1)S(1)} %copy-done.4), channel_id=1, source_target_pairs={{0,1},{1,2},{2,3},{3,0},{4,5},{5,6},{6,7},{7,4},{8,9},{9,10},{10,1... | collective-permute-start | bytes 1032200 | tf_op jit(solution)/shard_map/ppermute | solution.py:262
  79.2 0.0 copy-done.3
  79.2 8.8 %collective-permute-start.1 = (bf16[448,384]{1,0:T(8,128)(2,1)S(1)}, bf16[448,384]{1,0:T(8,128)(2,1)S(1)}, u32[]{:S(2)}, u32[]{:S(2)}) collective-permute-start(bf16[448,384]{1,0:T(8,128)(2,1)S(1)} %copy-done.3), channel_id=1, source_target_pairs={{0,2},{1,3},{2,0},{3,1},{4,6},{5,7},{6,4},{7,5},{8,10},{9,11},{10,... | collective-permute-start | bytes 1032200 | tf_op jit(solution)/shard_map/ppermute | solution.py:262
  88.0 0.0 copy-done.2
  88.0 4.3 %collective-permute-start.2 = (bf16[448,384]{1,0:T(8,128)(2,1)S(1)}, bf16[448,384]{1,0:T(8,128)(2,1)S(1)}, u32[]{:S(2)}, u32[]{:S(2)}) collective-permute-start(bf16[448,384]{1,0:T(8,128)(2,1)S(1)} %copy-done.2), channel_id=1, source_target_pairs={{0,3},{1,0},{2,1},{3,2},{4,7},{5,4},{6,5},{7,6},{8,11},{9,8},{10,9... | collective-permute-start | bytes 1032200 | tf_op jit(solution)/shard_map/ppermute | solution.py:262
  92.3 13.0 %collective-permute-done.second = bf16[448,384]{1,0:T(8,128)(2,1)S(1)} collective-permute-done((bf16[448,384]{1,0:T(8,128)(2,1)S(1)}, bf16[448,384]{1,0:T(8,128)(2,1)S(1)}, u32[]{:S(2)}, u32[]{:S(2)}) %collective-permute-start) | collective-permute-done | bytes 344096 | tf_op jit(solution)/shard_map/ppermute | solution.py:262
  105.3 21.7 %collective-permute-done.1.third = bf16[448,384]{1,0:T(8,128)(2,1)S(1)} collective-permute-done((bf16[448,384]{1,0:T(8,128)(2,1)S(1)}, bf16[448,384]{1,0:T(8,128)(2,1)S(1)}, u32[]{:S(2)}, u32[]{:S(2)}) %collective-permute-start.1) | collective-permute-done | bytes 344096 | tf_op jit(solution)/shard_map/ppermute | solution.py:262
  127.1 5.8 %collective-permute-done.2.fourth = bf16[448,384]{1,0:T(8,128)(2,1)S(1)} collective-permute-done((bf16[448,384]{1,0:T(8,128)(2,1)S(1)}, bf16[448,384]{1,0:T(8,128)(2,1)S(1)}, u32[]{:S(2)}, u32[]{:S(2)}) %collective-permute-start.2) | collective-permute-done | bytes 344096 | tf_op jit(solution)/shard_map/ppermute | solution.py:262
  132.9 0.0 copy-done.1
  132.9 2.6 %attend.1 = (bf16[1,256,384]{2,1,0:T(8,128)(2,1)}, bf16[64,384]{1,0:T(8,128)(2,1)}) custom-call(s32[1]{0:T(128)} %bitcast.place, bf16[448,384]{1,0:T(8,128)(2,1)S(1)} %copy-done.1, bf16[448,384]{1,0:T(8,128)(2,1)S(1)} %collective-permute-done.second, bf16[448,384]{1,0:T(8,128)(2,1)S(1)} %collective-permute-done.1.third, ...), custom_call_target="tpu_custom_call" | custom-call | tf_op jit(solution)/shard_map/attend/pallas_call | solution.py:264
  135.5 19.7 %all-gather = bf16[256,384]{1,0:T(8,128)(2,1)} all-gather(bf16[64,384]{1,0:T(8,128)(2,1)} %get-tuple-element.22), channel_id=2, replica_groups=mesh['x'=4,'y'=8,'zl'=3,'core'=2,'seq'=4] {'seq'}, dimensions={0}, use_global_device_ids=true | all-gather | bytes 245760 | tf_op jit(solution)/shard_map/all_gather | solution.py:268
  155.1 4.4 %embed.1.residual_in = f32[64,1408]{1,0:T(8,128)} custom-call(bf16[4,64,384]{2,1,0:T(8,128)(2,1)} %bitcast.8, bf16[1536,1408]{1,0:T(8,128)(2,1)} %embed_rows.1, f32[64,1408]{1,0:T(8,128)} %position_embed.1), custom_call_target="tpu_custom_call" | custom-call | tf_op jit(solution)/shard_map/embed/pallas_call | solution.py:269
  159.5 0.0 collective-permute-done.3.second.second_rows
  159.6 0.0 copy-start
  159.6 5.1 %forward.1 = (bf16[32,1408]{1,0:T(8,128)(2,1)}, bf16[32,1408]{1,0:T(8,128)(2,1)}, f32[64,768]{1,0:T(8,128)}) custom-call(s32[1]{0:T(128)} %bitcast.3.core, f32[64,1408]{1,0:T(8,128)} %embed.1.residual_in, f32[1,1408]{1,0:T(1,128)} %get-tuple-element.23.norm_gain, bf16[768,1408]{1,0:T(8,128)(2,1)} %bitcast.6.first_rows, ...), custom_call_target="tpu_custom_call" | custom-call | tf_op jit(solution)/shard_map/forward/pallas_call | solution.py:275
  164.7 0.0 copy-done
  164.7 4.1 %collective-permute-start.4 = (bf16[32,1408]{1,0:T(8,128)(2,1)}, bf16[32,1408]{1,0:T(8,128)(2,1)S(1)}, u32[]{:S(2)}, u32[]{:S(2)}) collective-permute-start(bf16[32,1408]{1,0:T(8,128)(2,1)} %get-tuple-element.25), channel_id=1, source_target_pairs={{0,1},{1,0},{2,3},{3,2},{4,5},{5,4},{6,7},{7,6},{8,9},{9,8},{10,11... | collective-permute-start | bytes 270344 | tf_op jit(solution)/shard_map/ppermute | solution.py:152
  168.8 4.7 %collective-permute-start.6 = (bf16[32,1408]{1,0:T(8,128)(2,1)}, bf16[32,1408]{1,0:T(8,128)(2,1)S(1)}, u32[]{:S(2)}, u32[]{:S(2)}) collective-permute-start(bf16[32,1408]{1,0:T(8,128)(2,1)} %get-tuple-element.26), channel_id=1, source_target_pairs={{0,3},{3,0},{1,2},{2,1},{4,7},{7,4},{5,6},{6,5},{8,11},{11,8},{9,1... | collective-permute-start | bytes 270344 | tf_op jit(solution)/shard_map/ppermute | solution.py:153
  173.5 0.0 collective-permute-done.4
  173.5 0.9 add_convert_fusion.1.b0
  174.5 7.4 %collective-permute-start.5 = (bf16[32,1408]{1,0:T(8,128)(2,1)S(1)}, bf16[32,1408]{1,0:T(8,128)(2,1)S(1)}, u32[]{:S(2)}, u32[]{:S(2)}) collective-permute-start(bf16[32,1408]{1,0:T(8,128)(2,1)S(1)} %add_convert_fusion.1.b0), channel_id=1, source_target_pairs={{0,3},{3,0},{1,2},{2,1},{4,7},{7,4},{5,6},{6,5},{8,11},{11,8},{9,1... | collective-permute-start | bytes 270344 | tf_op jit(solution)/shard_map/ppermute | solution.py:155
  181.9 0.0 collective-permute-done.6
  181.9 0.9 add_convert_fusion.b2
  182.8 1.9 collective-permute-start.7
  184.7 0.6 collective-permute-done.5.b1
  185.3 5.7 %collective-permute-done.7.b3 = bf16[32,1408]{1,0:T(8,128)(2,1)S(1)} collective-permute-done((bf16[32,1408]{1,0:T(8,128)(2,1)S(1)}, bf16[32,1408]{1,0:T(8,128)(2,1)S(1)}, u32[]{:S(2)}, u32[]{:S(2)}) %collective-permute-start.7) | collective-permute-done | bytes 90144 | tf_op jit(solution)/shard_map/ppermute | solution.py:155
  191.0 7.4 %backward.1 = (bf16[4,64,384]{2,1,0:T(8,128)(2,1)}, f32[1]{0:T(128)}) custom-call(s32[1]{0:T(128)} %bitcast.3.core, f32[64,1408]{1,0:T(8,128)} %embed.1.residual_in, bf16[32,1408]{1,0:T(8,128)(2,1)S(1)} %add_convert_fusion.1.b0, bf16[32,1408]{1,0:T(8,128)(2,1)S(1)} %collective-permute-done.5.b1, bf16[32,1408]{1,0:T(8,128)(2,1)S(1)} %add_convert_fusion.b2, ...), custom_call_target="tpu_custom_call" | custom-call | tf_op jit(solution)/shard_map/backward/pallas_call | solution.py:284
  198.4 18.1 %all_to_all.22.blocks = bf16[4,64,384]{2,1,0:T(8,128)(2,1)S(1)} all-to-all(bf16[4,64,384]{2,1,0:T(8,128)(2,1)} %get-tuple-element.29), channel_id=1, replica_groups=mesh['x'=4,'y'=8,'zl'=3,'core'=2,'seq'=4] {'seq'}, dimensions={0} | all-to-all | bytes 393216 | tf_op jit(solution)/shard_map/all_to_all | solution.py:296
  216.5 0.9 finish.1
  (2 shorter events, 0.1 us)
Async XLA Ops:
  3.3 11.5 %all-to-all-start = ((bf16[6,8,1408]{2,1,0:T(8,128)(2,1)}), bf16[6,8,1408]{2,1,0:T(8,128)(2,1)S(1)}, u32[]{:S(2)}, u32[]{:S(2)}) async-start(bf16[6,8,1408]{2,1,0:T(8,128)(2,1)} %get-tuple-element.24), calls=%async_computation | async-start | bytes 270336 | tf_op jit(solution)/shard_map/all_to_all | solution.py:250
  39.3 31.7 %copy-start.4 = (bf16[448,384]{1,0:T(8,128)(2,1)S(1)}, bf16[448,384]{1,0:T(8,128)(2,1)}, u32[]{:S(2)}) copy-start(bf16[448,384]{1,0:T(8,128)(2,1)} %get-tuple-element.18) | copy-start | bytes 1032196
  39.3 39.9 %copy-start.3 = (bf16[448,384]{1,0:T(8,128)(2,1)S(1)}, bf16[448,384]{1,0:T(8,128)(2,1)}, u32[]{:S(2)}) copy-start(bf16[448,384]{1,0:T(8,128)(2,1)} %get-tuple-element.19) | copy-start | bytes 1032196
  39.3 48.7 %copy-start.2 = (bf16[448,384]{1,0:T(8,128)(2,1)S(1)}, bf16[448,384]{1,0:T(8,128)(2,1)}, u32[]{:S(2)}) copy-start(bf16[448,384]{1,0:T(8,128)(2,1)} %get-tuple-element.20) | copy-start | bytes 1032196
  39.3 93.5 %copy-start.1 = (bf16[448,384]{1,0:T(8,128)(2,1)S(1)}, bf16[448,384]{1,0:T(8,128)(2,1)}, u32[]{:S(2)}) copy-start(bf16[448,384]{1,0:T(8,128)(2,1)} %get-tuple-element.17.first) | copy-start | bytes 1032196
  69.0 90.5 %collective-permute-start.3 = (bf16[768,1408]{1,0:T(8,128)(2,1)}, bf16[768,1408]{1,0:T(8,128)(2,1)S(1)}, u32[]{:S(2)}, u32[]{:S(2)}) collective-permute-start(bf16[768,1408]{1,0:T(8,128)(2,1)} %bitcast.6.first_rows), channel_id=1, source_target_pairs={{0,4},{4,0},{1,5},{5,1},{2,6},{6,2},{3,7},{7,3},{8,12},{12,8},{9,1... | collective-permute-start | bytes 6488072 | tf_op jit(solution)/shard_map/ppermute | solution.py:256
  71.0 34.3 %collective-permute-start = (bf16[448,384]{1,0:T(8,128)(2,1)S(1)}, bf16[448,384]{1,0:T(8,128)(2,1)S(1)}, u32[]{:S(2)}, u32[]{:S(2)}) collective-permute-start(bf16[448,384]{1,0:T(8,128)(2,1)S(1)} %copy-done.4), channel_id=1, source_target_pairs={{0,1},{1,2},{2,3},{3,0},{4,5},{5,6},{6,7},{7,4},{8,9},{9,10},{10,1... | collective-permute-start | bytes 1032200 | tf_op jit(solution)/shard_map/ppermute | solution.py:262
  79.2 47.9 %collective-permute-start.1 = (bf16[448,384]{1,0:T(8,128)(2,1)S(1)}, bf16[448,384]{1,0:T(8,128)(2,1)S(1)}, u32[]{:S(2)}, u32[]{:S(2)}) collective-permute-start(bf16[448,384]{1,0:T(8,128)(2,1)S(1)} %copy-done.3), channel_id=1, source_target_pairs={{0,2},{1,3},{2,0},{3,1},{4,6},{5,7},{6,4},{7,5},{8,10},{9,11},{10,... | collective-permute-start | bytes 1032200 | tf_op jit(solution)/shard_map/ppermute | solution.py:262
  88.0 44.8 %collective-permute-start.2 = (bf16[448,384]{1,0:T(8,128)(2,1)S(1)}, bf16[448,384]{1,0:T(8,128)(2,1)S(1)}, u32[]{:S(2)}, u32[]{:S(2)}) collective-permute-start(bf16[448,384]{1,0:T(8,128)(2,1)S(1)} %copy-done.2), channel_id=1, source_target_pairs={{0,3},{1,0},{2,1},{3,2},{4,7},{5,4},{6,5},{7,6},{8,11},{9,8},{10,9... | collective-permute-start | bytes 1032200 | tf_op jit(solution)/shard_map/ppermute | solution.py:262
  159.6 5.1 %copy-start = (bf16[768,1408]{1,0:T(8,128)(2,1)}, bf16[768,1408]{1,0:T(8,128)(2,1)S(1)}, u32[]{:S(2)}) copy-start(bf16[768,1408]{1,0:T(8,128)(2,1)S(1)} %collective-permute-done.3.second.second_rows) | copy-start | bytes 6488068
  164.7 8.9 %collective-permute-start.4 = (bf16[32,1408]{1,0:T(8,128)(2,1)}, bf16[32,1408]{1,0:T(8,128)(2,1)S(1)}, u32[]{:S(2)}, u32[]{:S(2)}) collective-permute-start(bf16[32,1408]{1,0:T(8,128)(2,1)} %get-tuple-element.25), channel_id=1, source_target_pairs={{0,1},{1,0},{2,3},{3,2},{4,5},{5,4},{6,7},{7,6},{8,9},{9,8},{10,11... | collective-permute-start | bytes 270344 | tf_op jit(solution)/shard_map/ppermute | solution.py:152
  168.8 13.1 %collective-permute-start.6 = (bf16[32,1408]{1,0:T(8,128)(2,1)}, bf16[32,1408]{1,0:T(8,128)(2,1)S(1)}, u32[]{:S(2)}, u32[]{:S(2)}) collective-permute-start(bf16[32,1408]{1,0:T(8,128)(2,1)} %get-tuple-element.26), channel_id=1, source_target_pairs={{0,3},{3,0},{1,2},{2,1},{4,7},{7,4},{5,6},{6,5},{8,11},{11,8},{9,1... | collective-permute-start | bytes 270344 | tf_op jit(solution)/shard_map/ppermute | solution.py:153
  174.5 10.8 %collective-permute-start.5 = (bf16[32,1408]{1,0:T(8,128)(2,1)S(1)}, bf16[32,1408]{1,0:T(8,128)(2,1)S(1)}, u32[]{:S(2)}, u32[]{:S(2)}) collective-permute-start(bf16[32,1408]{1,0:T(8,128)(2,1)S(1)} %add_convert_fusion.1.b0), channel_id=1, source_target_pairs={{0,3},{3,0},{1,2},{2,1},{4,7},{7,4},{5,6},{6,5},{8,11},{11,8},{9,1... | collective-permute-start | bytes 270344 | tf_op jit(solution)/shard_map/ppermute | solution.py:155
  182.8 8.2 %collective-permute-start.7 = (bf16[32,1408]{1,0:T(8,128)(2,1)S(1)}, bf16[32,1408]{1,0:T(8,128)(2,1)S(1)}, u32[]{:S(2)}, u32[]{:S(2)}) collective-permute-start(bf16[32,1408]{1,0:T(8,128)(2,1)S(1)} %add_convert_fusion.b2), channel_id=1, source_target_pairs={{0,1},{1,0},{2,3},{3,2},{4,5},{5,4},{6,7},{7,6},{8,9},{9,8},{10,11... | collective-permute-start | bytes 270344 | tf_op jit(solution)/shard_map/ppermute | solution.py:155

commit v5 on v4

--- a/solution.py
+++ b/solution.py
@@ -117,12 +117,9 @@
         compute(second, first)
 
 
-def forward_body(core, residual_in, norm_gain, first_rows, second, low, high, derivative_out, hidden, first, sem):
-    fetch = pltpu.make_async_copy(first_rows, first, sem)
-    fetch.start()
+def forward_body(core, residual_in, norm_gain, first, second, low, high, derivative_out, hidden):
     normed, _ = layer_stats(residual_in[...])
     hidden[...] = (normed * norm_gain[...]).astype(bf16)
-    fetch.wait()
 
     def compute(up, down):
         preact = contract_rows(hidden[...], up[...])
@@ -156,23 +153,16 @@
 
 
 def backward_body(
-    core, residual_in, b0, b1, b2, b3, norm_gain, direction_row, derivative, first_rows, second_rows, embed_rows,
-    blocks, reward, out_slope, part, first, second, embed_weight, sems,
+    core, residual_in, b0, b1, b2, b3, norm_gain, direction_row, derivative, first, second, embed_rows,
+    blocks, reward, out_slope, part, embed_weight, sem,
 ):
-    copies = [
-        pltpu.make_async_copy(first_rows, first, sems.at[0]),
-        pltpu.make_async_copy(second_rows, second, sems.at[1]),
-        pltpu.make_async_copy(embed_rows, embed_weight, sems.at[2]),
-    ]
-    for copy in copies:
-        copy.start()
+    fetch = pltpu.make_async_copy(embed_rows, embed_weight, sem)
+    fetch.start()
     residual_out = residual_in[...] + sum_halves((b0, b1, b2, b3))
     normed, inverse_std = layer_stats(residual_out)
     direction = direction_row[...]
     reward[0] = jnp.sum(normed * direction) * (1.0 / 64.0)
     out_slope[...] = layer_back(direction, normed, inverse_std)
-    copies[0].wait()
-    copies[1].wait()
 
     def compute(up, down):
         back_slope = contract_rows(out_slope[...].astype(bf16), down[...])
@@ -183,7 +173,7 @@
     normed, inverse_std = layer_stats(residual_in[...])
     share = layer_back(part[...] * norm_gain[...], normed, inverse_std)
     share = (share + 0.25 * out_slope[...]).astype(bf16)
-    copies[2].wait()
+    fetch.wait()
     for group in range(GROUPS):
         rows = slice(group * WIDTH, (group + 1) * WIDTH)
         blocks[group] = (0.25 * contract_rows(share, embed_weight[rows, :])).astype(bf16)
@@ -221,6 +211,7 @@
     return [pl.BlockSpec(memory_space=pltpu.VMEM)] * count
 
 
+room = pltpu.CompilerParams(vmem_limit_bytes=16 * 1024 * 1024)
 scalar_spec = pl.BlockSpec(memory_space=pltpu.SMEM)
 
 
@@ -255,7 +246,6 @@
     first = spread_to(mine, "x", 4).reshape(HIDDEN, EMB)
     second = lax.ppermute(first, "core", [(0, 1), (1, 0)])
 
-    first = in_hbm(first)
     received = [packed[0]]
     for step in (2, 1, 3):
         around = [(member, (member + step) % GROUPS) for member in range(GROUPS)]
@@ -269,29 +259,27 @@
     residual_in = pl.pallas_call(
         embed_body, out_shape=shape((64, EMB), f32),
         in_specs=[in_vmem(1)[0], *in_any(1), *in_vmem(1)], out_specs=pl.BlockSpec(memory_space=pltpu.VMEM),
-        scratch_shapes=[pltpu.VMEM((1536, EMB), bf16), pltpu.SemaphoreType.DMA((GROUPS,))], name="embed",
-    )(pooled, embed_weight, position_embed)
+        scratch_shapes=[pltpu.VMEM((1536, EMB), bf16), pltpu.SemaphoreType.DMA((GROUPS,))],
+        compiler_params=room, name="embed",
+    )(pooled, in_hbm(embed_weight), in_hbm(position_embed))
     half = shape((32, EMB), bf16)
     low, high, derivative = pl.pallas_call(
         forward_body, out_shape=(half, half, shape((64, HIDDEN), f32)),
-        in_specs=[scalar_spec, *in_vmem(2), *in_any(1), *in_vmem(1)], out_specs=tuple(in_vmem(3)),
-        scratch_shapes=[
-            pltpu.VMEM((64, EMB), bf16), pltpu.VMEM((HIDDEN, EMB), bf16), pltpu.SemaphoreType.DMA,
-        ],
-        name="forward",
-    )(core, residual_in, gain_row, first, held(second))
+        in_specs=[scalar_spec, *in_vmem(4)], out_specs=tuple(in_vmem(3)),
+        scratch_shapes=[pltpu.VMEM((64, EMB), bf16)], compiler_params=room, name="forward",
+    )(core, residual_in, gain_row, held(first), held(second))
     branch = group_sum(low, high)
     blocks, reward = pl.pallas_call(
         backward_body, out_shape=(shape((GROUPS, 64, WIDTH), bf16), shape((1,), f32)),
-        in_specs=[scalar_spec, *in_vmem(8), *in_any(3)], out_specs=(in_vmem(1)[0], scalar_spec),
+        in_specs=[scalar_spec, *in_vmem(10), *in_any(1)], out_specs=(in_vmem(1)[0], scalar_spec),
         scratch_shapes=[
-            pltpu.VMEM((64, EMB), f32), pltpu.VMEM((64, EMB), f32), pltpu.VMEM((HIDDEN, EMB), bf16),
-            pltpu.VMEM((HIDDEN, EMB), bf16), pltpu.VMEM((1536, EMB), bf16), pltpu.SemaphoreType.DMA((3,)),
+            pltpu.VMEM((64, EMB), f32), pltpu.VMEM((64, EMB), f32), pltpu.VMEM((1536, EMB), bf16),
+            pltpu.SemaphoreType.DMA,
         ],
-        name="backward",
+        compiler_params=room, name="backward",
     )(
-        core, residual_in, *map(held, branch), gain_row, direction_row, derivative, first, in_hbm(second),
-        embed_weight,
+        core, residual_in, *map(held, branch), gain_row, direction_row, derivative, held(first),
+        held(second), in_hbm(embed_weight),
     )
     blocks = lax.all_to_all(blocks, "seq", split_axis=0, concat_axis=0, tiled=True)
     gradient = pl.pallas_call(

time: 219 us -> 212 us (0.968)
  Pallas kernels: 23 us -> 18.6 us
  transfers between devices with their start and end apart: 9 -> 9, of which waited for: 6 -> 7; matrix products, arithmetic and copies ran while one was open for 1% -> 0% of each run, Pallas kernels for 3% -> 3%
where the time goes in v5:
time: 212 us; the launch traced here: 210 us
  blocking collectives  90.5 us (43%)
  waiting for transfers between devices  52.7 us (25%)
  starting transfers between devices  47.2 us (22%)
  Pallas kernels  18.6 us (9%)
    all_to_all x2, blocking collectives, spread_to(): return lax.all_to_all(copies, axes, split_axis=0, concat_axis=0, tiled=True)  53.1 us
    ppermute x3, waiting for transfers between devices, on_device(): received.append(lax.ppermute(packed[step], 'seq', around))  40.6 us
    ppermute x3, starting transfers between devices, on_device(): received.append(lax.ppermute(packed[step], 'seq', around))  22 us
    all_gather x1, blocking collectives, on_device(): pooled = lax.all_gather(pooled, 'seq', axis=0, tiled=False)  18.9 us
    all_to_all x1, blocking collectives, on_device(): lax.all_to_all(blocks, 'seq', split_axis=0, concat_axis=0, tiled=True)  18.5 us
    ppermute x1, starting transfers between devices, group_sum(): lax.ppermute(low, 'seq', outer)  6.24 us
    all_to_all x1, waiting for transfers between devices, on_device(): lax.all_to_all(copies, ('zl', 'core'), split_axis=0, concat_axis=0, tiled...  6.03 us
    pallas_call x1, Pallas kernels, on_device(): pl.pallas_call(backward_body, out_shape=(shape((GROUPS, 64, WIDTH), bf16)...  5.61 us
  transfers between devices with their start and end apart: 9, of which 7 were waited for; matrix products, arithmetic and copies ran while one was open for 0% of the time, Pallas kernels for 3%

profile of v5, /device:TPU:6, one launch (start us, length us, event | category | flops | bytes accessed | tf_op | source)
XLA Modules:
  0.0 210.2 jit_solution(10918766602528044671)
XLA Ops:
  0.6 2.6 %pack.1 = (bf16[448,384]{1,0:T(8,128)(2,1)}, bf16[448,384]{1,0:T(8,128)(2,1)}, bf16[448,384]{1,0:T(8,128)(2,1)}, bf16[448,384]{1,0:T(8,128)(2,1)}, f32[1,1408]{1...) custom-call(s32[1]{0:T(128)} %bitcast.place, bf16[1,64,1536]{2,1,0:T(8,128)(2,1)} %query.1, ...), custom_call_target="tpu_custom_call" | custom-call | tf_op jit(solution)/shard_map/pack/pallas_call | solution.py:229
  3.3 5.5 %all-to-all-start = ((bf16[6,8,1408]{2,1,0:T(8,128)(2,1)}), bf16[6,8,1408]{2,1,0:T(8,128)(2,1)S(1)}, u32[]{:S(2)}, u32[]{:S(2)}) async-start(bf16[6,8,1408]{2,1,0:T(8,128)(2,1)} %get-tuple-element.24), calls=%async_computation | async-start | bytes 270336 | tf_op jit(solution)/shard_map/all_to_all | solution.py:241
  8.7 6.0 %all-to-all-done = bf16[6,8,1408]{2,1,0:T(8,128)(2,1)S(1)} async-done(((bf16[6,8,1408]{2,1,0:T(8,128)(2,1)}), bf16[6,8,1408]{2,1,0:T(8,128)(2,1)S(1)}, u32[]{:S(2)}, u32[]{:S(2)}) %all-to-all-start) | async-done | bytes 135200 | tf_op jit(solution)/shard_map/all_to_all | solution.py:241
  14.8 0.1 slice_select_fusion
  14.9 24.2 %all_to_all.20 = bf16[8,24,1408]{2,1,0:T(8,128)(2,1)S(1)} all-to-all(bf16[8,24,1408]{2,1,0:T(8,128)(2,1)S(1)} %broadcast_in_dim.6), channel_id=1, replica_groups=mesh['x'=4,'y'=8,'zl'=3,'core'=2,'seq'=4] {'y'}, dimensions={0} | all-to-all | bytes 1081344 | tf_op jit(solution)/shard_map/all_to_all | solution.py:220
  39.1 0.2 broadcast_in_dim.15
  39.3 0.0 copy-start.5
  39.3 0.0 copy-start.4
  39.3 0.0 copy-start.3
  39.3 0.0 copy-start
  39.3 28.9 %all_to_all.21 = bf16[4,192,1408]{2,1,0:T(8,128)(2,1)S(1)} all-to-all(bf16[4,192,1408]{2,1,0:T(8,128)(2,1)S(1)} %broadcast_in_dim.15), channel_id=1, replica_groups=mesh['x'=4,'y'=8,'zl'=3,'core'=2,'seq'=4] {'x'}, dimensions={0} | all-to-all | bytes 4325376 | tf_op jit(solution)/shard_map/all_to_all | solution.py:220
  68.2 1.9 collective-permute-start.3
  70.2 0.0 copy-done.5
  70.2 8.9 %collective-permute-start = (bf16[448,384]{1,0:T(8,128)(2,1)S(1)}, bf16[448,384]{1,0:T(8,128)(2,1)S(1)}, u32[]{:S(2)}, u32[]{:S(2)}) collective-permute-start(bf16[448,384]{1,0:T(8,128)(2,1)S(1)} %copy-done.5), channel_id=1, source_target_pairs={{0,1},{1,2},{2,3},{3,0},{4,5},{5,6},{6,7},{7,4},{8,9},{9,10},{10,1... | collective-permute-start | bytes 1032200 | tf_op jit(solution)/shard_map/ppermute | solution.py:252
  79.1 0.0 copy-done.4
  79.1 8.8 %collective-permute-start.1 = (bf16[448,384]{1,0:T(8,128)(2,1)S(1)}, bf16[448,384]{1,0:T(8,128)(2,1)S(1)}, u32[]{:S(2)}, u32[]{:S(2)}) collective-permute-start(bf16[448,384]{1,0:T(8,128)(2,1)S(1)} %copy-done.4), channel_id=1, source_target_pairs={{0,2},{1,3},{2,0},{3,1},{4,6},{5,7},{6,4},{7,5},{8,10},{9,11},{10,... | collective-permute-start | bytes 1032200 | tf_op jit(solution)/shard_map/ppermute | solution.py:252
  87.9 0.0 copy-done.3
  87.9 4.3 %collective-permute-start.2 = (bf16[448,384]{1,0:T(8,128)(2,1)S(1)}, bf16[448,384]{1,0:T(8,128)(2,1)S(1)}, u32[]{:S(2)}, u32[]{:S(2)}) collective-permute-start(bf16[448,384]{1,0:T(8,128)(2,1)S(1)} %copy-done.3), channel_id=1, source_target_pairs={{0,3},{1,0},{2,1},{3,2},{4,7},{5,4},{6,5},{7,6},{8,11},{9,8},{10,9... | collective-permute-start | bytes 1032200 | tf_op jit(solution)/shard_map/ppermute | solution.py:252
  92.2 13.0 %collective-permute-done.second = bf16[448,384]{1,0:T(8,128)(2,1)S(1)} collective-permute-done((bf16[448,384]{1,0:T(8,128)(2,1)S(1)}, bf16[448,384]{1,0:T(8,128)(2,1)S(1)}, u32[]{:S(2)}, u32[]{:S(2)}) %collective-permute-start) | collective-permute-done | bytes 344096 | tf_op jit(solution)/shard_map/ppermute | solution.py:252
  105.2 21.8 %collective-permute-done.1.third = bf16[448,384]{1,0:T(8,128)(2,1)S(1)} collective-permute-done((bf16[448,384]{1,0:T(8,128)(2,1)S(1)}, bf16[448,384]{1,0:T(8,128)(2,1)S(1)}, u32[]{:S(2)}, u32[]{:S(2)}) %collective-permute-start.1) | collective-permute-done | bytes 344096 | tf_op jit(solution)/shard_map/ppermute | solution.py:252
  127.0 5.7 %collective-permute-done.2.fourth = bf16[448,384]{1,0:T(8,128)(2,1)S(1)} collective-permute-done((bf16[448,384]{1,0:T(8,128)(2,1)S(1)}, bf16[448,384]{1,0:T(8,128)(2,1)S(1)}, u32[]{:S(2)}, u32[]{:S(2)}) %collective-permute-start.2) | collective-permute-done | bytes 344096 | tf_op jit(solution)/shard_map/ppermute | solution.py:252
  132.8 0.0 copy-done
  132.8 2.6 %attend.1 = (bf16[1,256,384]{2,1,0:T(8,128)(2,1)}, bf16[64,384]{1,0:T(8,128)(2,1)}) custom-call(s32[1]{0:T(128)} %bitcast.place, bf16[448,384]{1,0:T(8,128)(2,1)S(1)} %copy-done, bf16[448,384]{1,0:T(8,128)(2,1)S(1)} %collective-permute-done.second, bf16[448,384]{1,0:T(8,128)(2,1)S(1)} %collective-permute-done.1.third, ...), custom_call_target="tpu_custom_call" | custom-call | tf_op jit(solution)/shard_map/attend/pallas_call | solution.py:254
  135.3 18.9 %all-gather = bf16[256,384]{1,0:T(8,128)(2,1)S(1)} all-gather(bf16[64,384]{1,0:T(8,128)(2,1)} %get-tuple-element.22), channel_id=2, replica_groups=mesh['x'=4,'y'=8,'zl'=3,'core'=2,'seq'=4] {'seq'}, dimensions={0}, use_global_device_ids=true | all-gather | bytes 245760 | tf_op jit(solution)/shard_map/all_gather | solution.py:258
  154.2 0.0 copy-start.1
  154.2 3.6 %embed.1.residual_in = f32[64,1408]{1,0:T(8,128)S(1)} custom-call(bf16[4,64,384]{2,1,0:T(8,128)(2,1)S(1)} %bitcast.10, bf16[1536,1408]{1,0:T(8,128)(2,1)} %embed_rows.1, f32[64,1408]{1,0:T(8,128)} %position_embed.1), custom_call_target="tpu_custom_call" | custom-call | tf_op jit(solution)/shard_map/embed/pallas_call | solution.py:259
  157.8 0.0 collective-permute-done.3.second
  157.8 0.0 copy-done.1
  157.8 0.0 copy-start.2
  157.8 3.3 %forward.1 = (bf16[32,1408]{1,0:T(8,128)(2,1)S(1)}, bf16[32,1408]{1,0:T(8,128)(2,1)S(1)}, f32[64,768]{1,0:T(8,128)S(1)}) custom-call(s32[1]{0:T(128)} %bitcast.3.core, f32[64,1408]{1,0:T(8,128)S(1)} %embed.1.residual_in, f32[1,1408]{1,0:T(1,128)S(1)} %copy-done.1, bf16[768,1408]{1,0:T(8,128)(2,1)S(1)} %bitcast.8, bf16[768,1408]{1,0:T(8,128)(2,1)} %collective-permute-done.3.second), custom_call_target="tpu_custom_call" | custom-call | tf_op jit(solution)/shard_map/forward/pallas_call | solution.py:266
  161.1 4.0 %collective-permute-start.4 = (bf16[32,1408]{1,0:T(8,128)(2,1)S(1)}, bf16[32,1408]{1,0:T(8,128)(2,1)S(1)}, u32[]{:S(2)}, u32[]{:S(2)}) collective-permute-start(bf16[32,1408]{1,0:T(8,128)(2,1)S(1)} %get-tuple-element.25), channel_id=1, source_target_pairs={{0,1},{1,0},{2,3},{3,2},{4,5},{5,4},{6,7},{7,6},{8,9},{9,8},{10,11... | collective-permute-start | bytes 270344 | tf_op jit(solution)/shard_map/ppermute | solution.py:149
  165.2 4.8 %collective-permute-start.6 = (bf16[32,1408]{1,0:T(8,128)(2,1)S(1)}, bf16[32,1408]{1,0:T(8,128)(2,1)S(1)}, u32[]{:S(2)}, u32[]{:S(2)}) collective-permute-start(bf16[32,1408]{1,0:T(8,128)(2,1)S(1)} %get-tuple-element.26), channel_id=1, source_target_pairs={{0,3},{3,0},{1,2},{2,1},{4,7},{7,4},{5,6},{6,5},{8,11},{11,8},{9,1... | collective-permute-start | bytes 270344 | tf_op jit(solution)/shard_map/ppermute | solution.py:150
  170.0 0.6 collective-permute-done.4
  170.7 6.2 %collective-permute-start.5 = (bf16[32,1408]{1,0:T(8,128)(2,1)S(1)}, bf16[32,1408]{1,0:T(8,128)(2,1)S(1)}, u32[]{:S(2)}, u32[]{:S(2)}) collective-permute-start(bf16[32,1408]{1,0:T(8,128)(2,1)S(1)} %add_convert_fusion.1.b0), channel_id=1, source_target_pairs={{0,3},{3,0},{1,2},{2,1},{4,7},{7,4},{5,6},{6,5},{8,11},{11,8},{9,1... | collective-permute-start | bytes 270344 | tf_op jit(solution)/shard_map/ppermute | solution.py:152
  176.9 0.0 collective-permute-done.6
  176.9 2.7 %collective-permute-start.7 = (bf16[32,1408]{1,0:T(8,128)(2,1)S(1)}, bf16[32,1408]{1,0:T(8,128)(2,1)S(1)}, u32[]{:S(2)}, u32[]{:S(2)}) collective-permute-start(bf16[32,1408]{1,0:T(8,128)(2,1)S(1)} %add_convert_fusion.b2), channel_id=1, source_target_pairs={{0,1},{1,0},{2,3},{3,2},{4,5},{5,4},{6,7},{7,6},{8,9},{9,8},{10,11... | collective-permute-start | bytes 270344 | tf_op jit(solution)/shard_map/ppermute | solution.py:152
  179.7 1.4 collective-permute-done.5.b1
  181.0 4.2 %collective-permute-done.7.b3 = bf16[32,1408]{1,0:T(8,128)(2,1)S(1)} collective-permute-done((bf16[32,1408]{1,0:T(8,128)(2,1)S(1)}, bf16[32,1408]{1,0:T(8,128)(2,1)S(1)}, u32[]{:S(2)}, u32[]{:S(2)}) %collective-permute-start.7) | collective-permute-done | bytes 90144 | tf_op jit(solution)/shard_map/ppermute | solution.py:152
  185.2 0.0 copy-done.2
  185.2 5.6 %backward.1 = (bf16[4,64,384]{2,1,0:T(8,128)(2,1)S(1)}, f32[1]{0:T(128)}) custom-call(s32[1]{0:T(128)} %bitcast.3.core, f32[64,1408]{1,0:T(8,128)S(1)} %embed.1.residual_in, bf16[32,1408]{1,0:T(8,128)(2,1)S(1)} %add_convert_fusion.1.b0, bf16[32,1408]{1,0:T(8,128)(2,1)S(1)} %collective-permute-done.5.b1, bf16[32,1408]{1,0:T(8,128)(2,1)S(1)} %add_convert_fusion.b2, ...), custom_call_target="tpu_custom_call" | custom-call | tf_op jit(solution)/shard_map/backward/pallas_call | solution.py:272
  190.8 18.5 %all_to_all.22.blocks = bf16[4,64,384]{2,1,0:T(8,128)(2,1)S(1)} all-to-all(bf16[4,64,384]{2,1,0:T(8,128)(2,1)S(1)} %get-tuple-element.29), channel_id=1, replica_groups=mesh['x'=4,'y'=8,'zl'=3,'core'=2,'seq'=4] {'seq'}, dimensions={0} | all-to-all | bytes 393216 | tf_op jit(solution)/shard_map/all_to_all | solution.py:284
  209.3 0.9 finish.1
  (4 shorter events, 0.1 us)
Async XLA Ops:
  3.3 11.5 %all-to-all-start = ((bf16[6,8,1408]{2,1,0:T(8,128)(2,1)}), bf16[6,8,1408]{2,1,0:T(8,128)(2,1)S(1)}, u32[]{:S(2)}, u32[]{:S(2)}) async-start(bf16[6,8,1408]{2,1,0:T(8,128)(2,1)} %get-tuple-element.24), calls=%async_computation | async-start | bytes 270336 | tf_op jit(solution)/shard_map/all_to_all | solution.py:241
  39.3 30.9 %copy-start.5 = (bf16[448,384]{1,0:T(8,128)(2,1)S(1)}, bf16[448,384]{1,0:T(8,128)(2,1)}, u32[]{:S(2)}) copy-start(bf16[448,384]{1,0:T(8,128)(2,1)} %get-tuple-element.18) | copy-start | bytes 1032196
  39.3 39.8 %copy-start.4 = (bf16[448,384]{1,0:T(8,128)(2,1)S(1)}, bf16[448,384]{1,0:T(8,128)(2,1)}, u32[]{:S(2)}) copy-start(bf16[448,384]{1,0:T(8,128)(2,1)} %get-tuple-element.19) | copy-start | bytes 1032196
  39.3 48.6 %copy-start.3 = (bf16[448,384]{1,0:T(8,128)(2,1)S(1)}, bf16[448,384]{1,0:T(8,128)(2,1)}, u32[]{:S(2)}) copy-start(bf16[448,384]{1,0:T(8,128)(2,1)} %get-tuple-element.20) | copy-start | bytes 1032196
  39.3 93.4 %copy-start = (bf16[448,384]{1,0:T(8,128)(2,1)S(1)}, bf16[448,384]{1,0:T(8,128)(2,1)}, u32[]{:S(2)}) copy-start(bf16[448,384]{1,0:T(8,128)(2,1)} %get-tuple-element.17.first) | copy-start | bytes 1032196
  68.2 89.5 %collective-permute-start.3 = (bf16[768,1408]{1,0:T(8,128)(2,1)S(1)}, bf16[768,1408]{1,0:T(8,128)(2,1)}, u32[]{:S(2)}, u32[]{:S(2)}) collective-permute-start(bf16[768,1408]{1,0:T(8,128)(2,1)S(1)} %bitcast.7), channel_id=1, source_target_pairs={{0,4},{4,0},{1,5},{5,1},{2,6},{6,2},{3,7},{7,3},{8,12},{12,8},{9,1... | collective-permute-start | bytes 6488072 | tf_op jit(solution)/shard_map/ppermute | solution.py:247
  70.2 35.0 %collective-permute-start = (bf16[448,384]{1,0:T(8,128)(2,1)S(1)}, bf16[448,384]{1,0:T(8,128)(2,1)S(1)}, u32[]{:S(2)}, u32[]{:S(2)}) collective-permute-start(bf16[448,384]{1,0:T(8,128)(2,1)S(1)} %copy-done.5), channel_id=1, source_target_pairs={{0,1},{1,2},{2,3},{3,0},{4,5},{5,6},{6,7},{7,4},{8,9},{9,10},{10,1... | collective-permute-start | bytes 1032200 | tf_op jit(solution)/shard_map/ppermute | solution.py:252
  79.1 47.9 %collective-permute-start.1 = (bf16[448,384]{1,0:T(8,128)(2,1)S(1)}, bf16[448,384]{1,0:T(8,128)(2,1)S(1)}, u32[]{:S(2)}, u32[]{:S(2)}) collective-permute-start(bf16[448,384]{1,0:T(8,128)(2,1)S(1)} %copy-done.4), channel_id=1, source_target_pairs={{0,2},{1,3},{2,0},{3,1},{4,6},{5,7},{6,4},{7,5},{8,10},{9,11},{10,... | collective-permute-start | bytes 1032200 | tf_op jit(solution)/shard_map/ppermute | solution.py:252
  87.9 44.8 %collective-permute-start.2 = (bf16[448,384]{1,0:T(8,128)(2,1)S(1)}, bf16[448,384]{1,0:T(8,128)(2,1)S(1)}, u32[]{:S(2)}, u32[]{:S(2)}) collective-permute-start(bf16[448,384]{1,0:T(8,128)(2,1)S(1)} %copy-done.3), channel_id=1, source_target_pairs={{0,3},{1,0},{2,1},{3,2},{4,7},{5,4},{6,5},{7,6},{8,11},{9,8},{10,9... | collective-permute-start | bytes 1032200 | tf_op jit(solution)/shard_map/ppermute | solution.py:252
  154.2 3.6 %copy-start.1 = (f32[1,1408]{1,0:T(1,128)S(1)}, f32[1,1408]{1,0:T(1,128)}, u32[]{:S(2)}) copy-start(f32[1,1408]{1,0:T(1,128)} %get-tuple-element.23.norm_gain) | copy-start | bytes 16900
  157.8 27.4 %copy-start.2 = (f32[1,1408]{1,0:T(1,128)S(1)}, f32[1,1408]{1,0:T(1,128)}, u32[]{:S(2)}) copy-start(f32[1,1408]{1,0:T(1,128)} %get-tuple-element.27.direction_row) | copy-start | bytes 16900
  161.1 9.5 %collective-permute-start.4 = (bf16[32,1408]{1,0:T(8,128)(2,1)S(1)}, bf16[32,1408]{1,0:T(8,128)(2,1)S(1)}, u32[]{:S(2)}, u32[]{:S(2)}) collective-permute-start(bf16[32,1408]{1,0:T(8,128)(2,1)S(1)} %get-tuple-element.25), channel_id=1, source_target_pairs={{0,1},{1,0},{2,3},{3,2},{4,5},{5,4},{6,7},{7,6},{8,9},{9,8},{10,11... | collective-permute-start | bytes 270344 | tf_op jit(solution)/shard_map/ppermute | solution.py:149
  165.2 11.7 %collective-permute-start.6 = (bf16[32,1408]{1,0:T(8,128)(2,1)S(1)}, bf16[32,1408]{1,0:T(8,128)(2,1)S(1)}, u32[]{:S(2)}, u32[]{:S(2)}) collective-permute-start(bf16[32,1408]{1,0:T(8,128)(2,1)S(1)} %get-tuple-element.26), channel_id=1, source_target_pairs={{0,3},{3,0},{1,2},{2,1},{4,7},{7,4},{5,6},{6,5},{8,11},{11,8},{9,1... | collective-permute-start | bytes 270344 | tf_op jit(solution)/shard_map/ppermute | solution.py:150
  170.7 10.4 %collective-permute-start.5 = (bf16[32,1408]{1,0:T(8,128)(2,1)S(1)}, bf16[32,1408]{1,0:T(8,128)(2,1)S(1)}, u32[]{:S(2)}, u32[]{:S(2)}) collective-permute-start(bf16[32,1408]{1,0:T(8,128)(2,1)S(1)} %add_convert_fusion.1.b0), channel_id=1, source_target_pairs={{0,3},{3,0},{1,2},{2,1},{4,7},{7,4},{5,6},{6,5},{8,11},{11,8},{9,1... | collective-permute-start | bytes 270344 | tf_op jit(solution)/shard_map/ppermute | solution.py:152
  176.9 8.3 %collective-permute-start.7 = (bf16[32,1408]{1,0:T(8,128)(2,1)S(1)}, bf16[32,1408]{1,0:T(8,128)(2,1)S(1)}, u32[]{:S(2)}, u32[]{:S(2)}) collective-permute-start(bf16[32,1408]{1,0:T(8,128)(2,1)S(1)} %add_convert_fusion.b2), channel_id=1, source_target_pairs={{0,1},{1,0},{2,3},{3,2},{4,5},{5,4},{6,7},{7,6},{8,9},{9,8},{10,11... | collective-permute-start | bytes 270344 | tf_op jit(solution)/shard_map/ppermute | solution.py:152

commit v6 on v5

--- a/solution.py
+++ b/solution.py
@@ -232,10 +232,11 @@
             *(shape((ROWS, WIDTH), bf16),) * GROUPS, shape((1, EMB), f32), shape((1, EMB), f32),
             shape((6, 8, EMB), bf16),
         ),
-        in_specs=[scalar_spec, *in_vmem(10)], out_specs=tuple(in_vmem(7)), name="pack",
+        in_specs=[scalar_spec, *in_vmem(10)], out_specs=tuple(in_vmem(7)), compiler_params=room, name="pack",
     )(
-        group, image_query, image_key, image_value, text_key, text_value, norm_gain, final_gain,
-        reward_direction, up_weight, down_weight,
+        group,
+        *map(in_hbm, (image_query, image_key, image_value, text_key, text_value, norm_gain, final_gain)),
+        in_hbm(reward_direction), in_hbm(up_weight), in_hbm(down_weight),
     )
     *packed, gain_row, direction_row, copies = packed
     nearby = lax.all_to_all(copies, ("zl", "core"), split_axis=0, concat_axis=0, tiled=True)
@@ -253,8 +254,8 @@
     received = [received[0], received[2], received[1], received[3]]
     attended, pooled = pl.pallas_call(
         attend_body, out_shape=(shape((1, 256, WIDTH), bf16), shape((64, WIDTH), bf16)),
-        in_specs=[scalar_spec, *in_vmem(6)], out_specs=tuple(in_vmem(2)), name="attend",
-    )(group, *map(held, received), query_gain.reshape(1, HEAD), key_gain.reshape(1, HEAD))
+        in_specs=[scalar_spec, *in_vmem(6)], out_specs=tuple(in_vmem(2)), compiler_params=room, name="attend",
+    )(group, *map(held, received), in_hbm(query_gain.reshape(1, HEAD)), in_hbm(key_gain.reshape(1, HEAD)))
     pooled = lax.all_gather(pooled, "seq", axis=0, tiled=False)
     residual_in = pl.pallas_call(
         embed_body, out_shape=shape((64, EMB), f32),
@@ -284,7 +285,7 @@
     blocks = lax.all_to_all(blocks, "seq", split_axis=0, concat_axis=0, tiled=True)
     gradient = pl.pallas_call(
         finish_body, out_shape=shape((1, 256, WIDTH), bf16), in_specs=in_vmem(1),
-        out_specs=pl.BlockSpec(memory_space=pltpu.VMEM), name="finish",
+        out_specs=pl.BlockSpec(memory_space=pltpu.VMEM), compiler_params=room, name="finish",
     )(held(blocks))
     return (attended, gradient, reward)
 

time: 212 us -> 206 us (0.972)
  Pallas kernels: 18.6 us -> 14.6 us
  transfers between devices with their start and end apart: 9 -> 9, of which waited for: 7 -> 5; matrix products, arithmetic and copies ran while one was open for 0% -> 0% of each run, Pallas kernels for 3% -> 3%
where the time goes in v6:
time: 206 us; the launch traced here: 205 us
  blocking collectives  88.9 us (43%)
  waiting for transfers between devices  51.4 us (25%)
  starting transfers between devices  48.6 us (24%)
  Pallas kernels  14.6 us (7%)
    all_to_all x2, blocking collectives, spread_to(): return lax.all_to_all(copies, axes, split_axis=0, concat_axis=0, tiled=True)  53 us
    ppermute x3, waiting for transfers between devices, on_device(): received.append(lax.ppermute(packed[step], 'seq', around))  40.6 us
    ppermute x3, starting transfers between devices, on_device(): received.append(lax.ppermute(packed[step], 'seq', around))  22 us
    all_gather x1, blocking collectives, on_device(): pooled = lax.all_gather(pooled, 'seq', axis=0, tiled=False)  18.8 us
    all_to_all x1, blocking collectives, on_device(): lax.all_to_all(blocks, 'seq', split_axis=0, concat_axis=0, tiled=True)  17.1 us
    ppermute x1, starting transfers between devices, group_sum(): lax.ppermute(low, 'seq', outer)  6.92 us
    all_to_all x1, waiting for transfers between devices, on_device(): lax.all_to_all(copies, ('zl', 'core'), split_axis=0, concat_axis=0, tiled...  6.03 us
    all_to_all x1, starting transfers between devices, on_device(): lax.all_to_all(copies, ('zl', 'core'), split_axis=0, concat_axis=0, tiled...  5.45 us
  transfers between devices with their start and end apart: 9, of which 5 were waited for; matrix products, arithmetic and copies ran while one was open for 0% of the time, Pallas kernels for 3%

profile of v6, /device:TPU:6, one launch (start us, length us, event | category | flops | bytes accessed | tf_op | source)
XLA Modules:
  0.0 204.6 jit_solution(4764918056374169163)
XLA Ops:
  0.6 2.2 %pack.1 = (bf16[448,384]{1,0:T(8,128)(2,1)S(1)}, bf16[448,384]{1,0:T(8,128)(2,1)S(1)}, bf16[448,384]{1,0:T(8,128)(2,1)S(1)}, bf16[448,384]{1,0:T(8,128)(2,1)S(1)...) custom-call(s32[1]{0:T(128)} %bitcast.place, bf16[1,64,1536]{2,1,0:T(8,128)(2,1)} %query.1, ...), custom_call_target="tpu_custom_call" | custom-call | tf_op jit(solution)/shard_map/pack/pallas_call | solution.py:229
  2.8 5.5 %all-to-all-start = ((bf16[6,8,1408]{2,1,0:T(8,128)(2,1)}), bf16[6,8,1408]{2,1,0:T(8,128)(2,1)S(1)}, u32[]{:S(2)}, u32[]{:S(2)}) async-start(bf16[6,8,1408]{2,1,0:T(8,128)(2,1)} %get-tuple-element.24), calls=%async_computation | async-start | bytes 270336 | tf_op jit(solution)/shard_map/all_to_all | solution.py:242
  8.3 6.0 %all-to-all-done = bf16[6,8,1408]{2,1,0:T(8,128)(2,1)S(1)} async-done(((bf16[6,8,1408]{2,1,0:T(8,128)(2,1)}), bf16[6,8,1408]{2,1,0:T(8,128)(2,1)S(1)}, u32[]{:S(2)}, u32[]{:S(2)}) %all-to-all-start) | async-done | bytes 135200 | tf_op jit(solution)/shard_map/all_to_all | solution.py:242
  14.3 0.1 slice_select_fusion
  14.4 24.2 %all_to_all.20 = bf16[8,24,1408]{2,1,0:T(8,128)(2,1)S(1)} all-to-all(bf16[8,24,1408]{2,1,0:T(8,128)(2,1)S(1)} %broadcast_in_dim.6), channel_id=1, replica_groups=mesh['x'=4,'y'=8,'zl'=3,'core'=2,'seq'=4] {'y'}, dimensions={0} | all-to-all | bytes 1081344 | tf_op jit(solution)/shard_map/all_to_all | solution.py:220
  38.7 0.2 broadcast_in_dim.15
  38.8 28.8 %all_to_all.21 = bf16[4,192,1408]{2,1,0:T(8,128)(2,1)S(1)} all-to-all(bf16[4,192,1408]{2,1,0:T(8,128)(2,1)S(1)} %broadcast_in_dim.15), channel_id=1, replica_groups=mesh['x'=4,'y'=8,'zl'=3,'core'=2,'seq'=4] {'x'}, dimensions={0} | all-to-all | bytes 4325376 | tf_op jit(solution)/shard_map/all_to_all | solution.py:220
  67.6 1.9 collective-permute-start.3
  69.5 8.9 %collective-permute-start = (bf16[448,384]{1,0:T(8,128)(2,1)S(1)}, bf16[448,384]{1,0:T(8,128)(2,1)S(1)}, u32[]{:S(2)}, u32[]{:S(2)}) collective-permute-start(bf16[448,384]{1,0:T(8,128)(2,1)S(1)} %get-tuple-element.18), channel_id=1, source_target_pairs={{0,1},{1,2},{2,3},{3,0},{4,5},{5,6},{6,7},{7,4},{8,9},{9,10},{10,1... | collective-permute-start | bytes 1032200 | tf_op jit(solution)/shard_map/ppermute | solution.py:253
  78.4 8.8 %collective-permute-start.1 = (bf16[448,384]{1,0:T(8,128)(2,1)S(1)}, bf16[448,384]{1,0:T(8,128)(2,1)S(1)}, u32[]{:S(2)}, u32[]{:S(2)}) collective-permute-start(bf16[448,384]{1,0:T(8,128)(2,1)S(1)} %get-tuple-element.19), channel_id=1, source_target_pairs={{0,2},{1,3},{2,0},{3,1},{4,6},{5,7},{6,4},{7,5},{8,10},{9,11},{10,... | collective-permute-start | bytes 1032200 | tf_op jit(solution)/shard_map/ppermute | solution.py:253
  87.3 4.3 %collective-permute-start.2 = (bf16[448,384]{1,0:T(8,128)(2,1)S(1)}, bf16[448,384]{1,0:T(8,128)(2,1)S(1)}, u32[]{:S(2)}, u32[]{:S(2)}) collective-permute-start(bf16[448,384]{1,0:T(8,128)(2,1)S(1)} %get-tuple-element.20), channel_id=1, source_target_pairs={{0,3},{1,0},{2,1},{3,2},{4,7},{5,4},{6,5},{7,6},{8,11},{9,8},{10,9... | collective-permute-start | bytes 1032200 | tf_op jit(solution)/shard_map/ppermute | solution.py:253
  91.5 13.0 %collective-permute-done.second = bf16[448,384]{1,0:T(8,128)(2,1)S(1)} collective-permute-done((bf16[448,384]{1,0:T(8,128)(2,1)S(1)}, bf16[448,384]{1,0:T(8,128)(2,1)S(1)}, u32[]{:S(2)}, u32[]{:S(2)}) %collective-permute-start) | collective-permute-done | bytes 344096 | tf_op jit(solution)/shard_map/ppermute | solution.py:253
  104.5 20.8 %collective-permute-done.1.third = bf16[448,384]{1,0:T(8,128)(2,1)S(1)} collective-permute-done((bf16[448,384]{1,0:T(8,128)(2,1)S(1)}, bf16[448,384]{1,0:T(8,128)(2,1)S(1)}, u32[]{:S(2)}, u32[]{:S(2)}) %collective-permute-start.1) | collective-permute-done | bytes 344096 | tf_op jit(solution)/shard_map/ppermute | solution.py:253
  125.3 6.8 %collective-permute-done.2.fourth = bf16[448,384]{1,0:T(8,128)(2,1)S(1)} collective-permute-done((bf16[448,384]{1,0:T(8,128)(2,1)S(1)}, bf16[448,384]{1,0:T(8,128)(2,1)S(1)}, u32[]{:S(2)}, u32[]{:S(2)}) %collective-permute-start.2) | collective-permute-done | bytes 344096 | tf_op jit(solution)/shard_map/ppermute | solution.py:253
  132.1 2.5 %attend.1 = (bf16[1,256,384]{2,1,0:T(8,128)(2,1)}, bf16[64,384]{1,0:T(8,128)(2,1)S(1)}) custom-call(s32[1]{0:T(128)} %bitcast.place, bf16[448,384]{1,0:T(8,128)(2,1)S(1)} %get-tuple-element.17.first, bf16[448,384]{1,0:T(8,128)(2,1)S(1)} %collective-permute-done.second, bf16[448,384]{1,0:T(8,128)(2,1)S(1)} %collective-permute-done.1.third, ...), custom_call_target="tpu_custom_call" | custom-call | tf_op jit(solution)/shard_map/attend/pallas_call | solution.py:255
  134.6 18.8 %all-gather = bf16[256,384]{1,0:T(8,128)(2,1)S(1)} all-gather(bf16[64,384]{1,0:T(8,128)(2,1)S(1)} %get-tuple-element.22), channel_id=2, replica_groups=mesh['x'=4,'y'=8,'zl'=3,'core'=2,'seq'=4] {'seq'}, dimensions={0}, use_global_device_ids=true | all-gather | bytes 245760 | tf_op jit(solution)/shard_map/all_gather | solution.py:259
  153.4 3.6 %embed.1.residual_in = f32[64,1408]{1,0:T(8,128)S(1)} custom-call(bf16[4,64,384]{2,1,0:T(8,128)(2,1)S(1)} %bitcast.10, bf16[1536,1408]{1,0:T(8,128)(2,1)} %embed_rows.1, f32[64,1408]{1,0:T(8,128)} %position_embed.1), custom_call_target="tpu_custom_call" | custom-call | tf_op jit(solution)/shard_map/embed/pallas_call | solution.py:260
  157.0 0.0 collective-permute-done.3.second
  157.0 1.7 forward.1
  158.7 3.9 %collective-permute-start.4 = (bf16[32,1408]{1,0:T(8,128)(2,1)S(1)}, bf16[32,1408]{1,0:T(8,128)(2,1)S(1)}, u32[]{:S(2)}, u32[]{:S(2)}) collective-permute-start(bf16[32,1408]{1,0:T(8,128)(2,1)S(1)} %get-tuple-element.25), channel_id=1, source_target_pairs={{0,1},{1,0},{2,3},{3,2},{4,5},{5,4},{6,7},{7,6},{8,9},{9,8},{10,11... | collective-permute-start | bytes 270344 | tf_op jit(solution)/shard_map/ppermute | solution.py:149
  162.7 4.9 %collective-permute-start.6 = (bf16[32,1408]{1,0:T(8,128)(2,1)S(1)}, bf16[32,1408]{1,0:T(8,128)(2,1)S(1)}, u32[]{:S(2)}, u32[]{:S(2)}) collective-permute-start(bf16[32,1408]{1,0:T(8,128)(2,1)S(1)} %get-tuple-element.26), channel_id=1, source_target_pairs={{0,3},{3,0},{1,2},{2,1},{4,7},{7,4},{5,6},{6,5},{8,11},{11,8},{9,1... | collective-permute-start | bytes 270344 | tf_op jit(solution)/shard_map/ppermute | solution.py:150
  167.6 0.0 collective-permute-done.4
  167.6 6.9 %collective-permute-start.5 = (bf16[32,1408]{1,0:T(8,128)(2,1)S(1)}, bf16[32,1408]{1,0:T(8,128)(2,1)S(1)}, u32[]{:S(2)}, u32[]{:S(2)}) collective-permute-start(bf16[32,1408]{1,0:T(8,128)(2,1)S(1)} %add_convert_fusion.1.b0), channel_id=1, source_target_pairs={{0,3},{3,0},{1,2},{2,1},{4,7},{7,4},{5,6},{6,5},{8,11},{11,8},{9,1... | collective-permute-start | bytes 270344 | tf_op jit(solution)/shard_map/ppermute | solution.py:152
  174.6 0.0 collective-permute-done.6
  174.6 3.5 %collective-permute-start.7 = (bf16[32,1408]{1,0:T(8,128)(2,1)S(1)}, bf16[32,1408]{1,0:T(8,128)(2,1)S(1)}, u32[]{:S(2)}, u32[]{:S(2)}) collective-permute-start(bf16[32,1408]{1,0:T(8,128)(2,1)S(1)} %add_convert_fusion.b2), channel_id=1, source_target_pairs={{0,1},{1,0},{2,3},{3,2},{4,5},{5,4},{6,7},{7,6},{8,9},{9,8},{10,11... | collective-permute-start | bytes 270344 | tf_op jit(solution)/shard_map/ppermute | solution.py:152
  178.1 0.0 collective-permute-done.5.b1
  178.1 4.8 %collective-permute-done.7.b3 = bf16[32,1408]{1,0:T(8,128)(2,1)S(1)} collective-permute-done((bf16[32,1408]{1,0:T(8,128)(2,1)S(1)}, bf16[32,1408]{1,0:T(8,128)(2,1)S(1)}, u32[]{:S(2)}, u32[]{:S(2)}) %collective-permute-start.7) | collective-permute-done | bytes 90144 | tf_op jit(solution)/shard_map/ppermute | solution.py:152
  182.9 3.7 %backward.1 = (bf16[4,64,384]{2,1,0:T(8,128)(2,1)S(1)}, f32[1]{0:T(128)}) custom-call(s32[1]{0:T(128)} %bitcast.3.core, f32[64,1408]{1,0:T(8,128)S(1)} %embed.1.residual_in, bf16[32,1408]{1,0:T(8,128)(2,1)S(1)} %add_convert_fusion.1.b0, bf16[32,1408]{1,0:T(8,128)(2,1)S(1)} %collective-permute-done.5.b1, bf16[32,1408]{1,0:T(8,128)(2,1)S(1)} %add_convert_fusion.b2, ...), custom_call_target="tpu_custom_call" | custom-call | tf_op jit(solution)/shard_map/backward/pallas_call | solution.py:273
  186.6 17.1 %all_to_all.22.blocks = bf16[4,64,384]{2,1,0:T(8,128)(2,1)S(1)} all-to-all(bf16[4,64,384]{2,1,0:T(8,128)(2,1)S(1)} %get-tuple-element.29), channel_id=1, replica_groups=mesh['x'=4,'y'=8,'zl'=3,'core'=2,'seq'=4] {'seq'}, dimensions={0} | all-to-all | bytes 393216 | tf_op jit(solution)/shard_map/all_to_all | solution.py:285
  203.7 0.9 finish.1
  (4 shorter events, 0.1 us)
Async XLA Ops:
  2.8 11.5 %all-to-all-start = ((bf16[6,8,1408]{2,1,0:T(8,128)(2,1)}), bf16[6,8,1408]{2,1,0:T(8,128)(2,1)S(1)}, u32[]{:S(2)}, u32[]{:S(2)}) async-start(bf16[6,8,1408]{2,1,0:T(8,128)(2,1)} %get-tuple-element.24), calls=%async_computation | async-start | bytes 270336 | tf_op jit(solution)/shard_map/all_to_all | solution.py:242
  67.6 89.4 %collective-permute-start.3 = (bf16[768,1408]{1,0:T(8,128)(2,1)S(1)}, bf16[768,1408]{1,0:T(8,128)(2,1)S(1)}, u32[]{:S(2)}, u32[]{:S(2)}) collective-permute-start(bf16[768,1408]{1,0:T(8,128)(2,1)S(1)} %bitcast.7), channel_id=1, source_target_pairs={{0,4},{4,0},{1,5},{5,1},{2,6},{6,2},{3,7},{7,3},{8,12},{12,8},{9,1... | collective-permute-start | bytes 6488072 | tf_op jit(solution)/shard_map/ppermute | solution.py:248
  69.5 35.0 %collective-permute-start = (bf16[448,384]{1,0:T(8,128)(2,1)S(1)}, bf16[448,384]{1,0:T(8,128)(2,1)S(1)}, u32[]{:S(2)}, u32[]{:S(2)}) collective-permute-start(bf16[448,384]{1,0:T(8,128)(2,1)S(1)} %get-tuple-element.18), channel_id=1, source_target_pairs={{0,1},{1,2},{2,3},{3,0},{4,5},{5,6},{6,7},{7,4},{8,9},{9,10},{10,1... | collective-permute-start | bytes 1032200 | tf_op jit(solution)/shard_map/ppermute | solution.py:253
  78.4 46.9 %collective-permute-start.1 = (bf16[448,384]{1,0:T(8,128)(2,1)S(1)}, bf16[448,384]{1,0:T(8,128)(2,1)S(1)}, u32[]{:S(2)}, u32[]{:S(2)}) collective-permute-start(bf16[448,384]{1,0:T(8,128)(2,1)S(1)} %get-tuple-element.19), channel_id=1, source_target_pairs={{0,2},{1,3},{2,0},{3,1},{4,6},{5,7},{6,4},{7,5},{8,10},{9,11},{10,... | collective-permute-start | bytes 1032200 | tf_op jit(solution)/shard_map/ppermute | solution.py:253
  87.3 44.8 %collective-permute-start.2 = (bf16[448,384]{1,0:T(8,128)(2,1)S(1)}, bf16[448,384]{1,0:T(8,128)(2,1)S(1)}, u32[]{:S(2)}, u32[]{:S(2)}) collective-permute-start(bf16[448,384]{1,0:T(8,128)(2,1)S(1)} %get-tuple-element.20), channel_id=1, source_target_pairs={{0,3},{1,0},{2,1},{3,2},{4,7},{5,4},{6,5},{7,6},{8,11},{9,8},{10,9... | collective-permute-start | bytes 1032200 | tf_op jit(solution)/shard_map/ppermute | solution.py:253
  158.7 8.9 %collective-permute-start.4 = (bf16[32,1408]{1,0:T(8,128)(2,1)S(1)}, bf16[32,1408]{1,0:T(8,128)(2,1)S(1)}, u32[]{:S(2)}, u32[]{:S(2)}) collective-permute-start(bf16[32,1408]{1,0:T(8,128)(2,1)S(1)} %get-tuple-element.25), channel_id=1, source_target_pairs={{0,1},{1,0},{2,3},{3,2},{4,5},{5,4},{6,7},{7,6},{8,9},{9,8},{10,11... | collective-permute-start | bytes 270344 | tf_op jit(solution)/shard_map/ppermute | solution.py:149
  162.7 11.9 %collective-permute-start.6 = (bf16[32,1408]{1,0:T(8,128)(2,1)S(1)}, bf16[32,1408]{1,0:T(8,128)(2,1)S(1)}, u32[]{:S(2)}, u32[]{:S(2)}) collective-permute-start(bf16[32,1408]{1,0:T(8,128)(2,1)S(1)} %get-tuple-element.26), channel_id=1, source_target_pairs={{0,3},{3,0},{1,2},{2,1},{4,7},{7,4},{5,6},{6,5},{8,11},{11,8},{9,1... | collective-permute-start | bytes 270344 | tf_op jit(solution)/shard_map/ppermute | solution.py:150
  167.6 10.5 %collective-permute-start.5 = (bf16[32,1408]{1,0:T(8,128)(2,1)S(1)}, bf16[32,1408]{1,0:T(8,128)(2,1)S(1)}, u32[]{:S(2)}, u32[]{:S(2)}) collective-permute-start(bf16[32,1408]{1,0:T(8,128)(2,1)S(1)} %add_convert_fusion.1.b0), channel_id=1, source_target_pairs={{0,3},{3,0},{1,2},{2,1},{4,7},{7,4},{5,6},{6,5},{8,11},{11,8},{9,1... | collective-permute-start | bytes 270344 | tf_op jit(solution)/shard_map/ppermute | solution.py:152
  174.6 8.3 %collective-permute-start.7 = (bf16[32,1408]{1,0:T(8,128)(2,1)S(1)}, bf16[32,1408]{1,0:T(8,128)(2,1)S(1)}, u32[]{:S(2)}, u32[]{:S(2)}) collective-permute-start(bf16[32,1408]{1,0:T(8,128)(2,1)S(1)} %add_convert_fusion.b2), channel_id=1, source_target_pairs={{0,1},{1,0},{2,3},{3,2},{4,5},{5,4},{6,7},{7,6},{8,9},{9,8},{10,11... | collective-permute-start | bytes 270344 | tf_op jit(solution)/shard_map/ppermute | solution.py:152
